TPU v7x, 32 devices: a whole 2x2x4 slice. The times are simulated.
32 devices in a mesh: dp: 4 (over y, x), seq: 8 (over z, core).
Axes of the slice: x: 2, y: 2, z: 4, core: 2. Of those that a mesh axis runs over, the one named last changes fastest.
Arguments:
- inputs: bfloat16 [2, 4, 1024, 1024], P(None, 'dp', 'seq'), may hold values from -6 to 6
- variate_ids: int32 [2, 4, 1024], P(None, 'dp', 'seq'), may hold values from 0 to 7
- time_ids: int32 [2, 4, 1024], P(None, 'dp', 'seq'), may hold values from 0 to 1023
- attn_gain: float32 [1024], P(('dp', 'seq')), may hold values from 0.5 to 1.5
- query_weight: float32 [1024, 1024], P(('dp', 'seq')), may hold values from -0.1875 to 0.1875
- key_weight: float32 [1024, 1024], P(('dp', 'seq')), may hold values from -0.1875 to 0.1875
- value_weight: float32 [1024, 1024], P(('dp', 'seq')), may hold values from -0.1875 to 0.1875
- out_weight: float32 [1024, 1024], P(('dp', 'seq')), may hold values from -3 to 3
- query_gain: float32 [64], replicated, may hold values from 0.1 to 1.9
- key_gain: float32 [64], replicated, may hold values from 0.1 to 1.9
- variate_bias: float32 [2, 16], replicated, may hold values from -3 to 3
- ffn_gain: float32 [1024], P(('dp', 'seq')), may hold values from 0.5 to 1.5
- gate_weight: float32 [4096, 1024], P(('dp', 'seq')), may hold values from -0.1875 to 0.1875
- up_weight: float32 [4096, 1024], P(('dp', 'seq')), may hold values from -0.1875 to 0.1875
- down_weight: float32 [4096, 1024], P(('dp', 'seq')), may hold values from -0.09375 to 0.09375
- out_grad: bfloat16 [2, 4, 1024, 1024], P(None, 'dp', 'seq'), may hold values from -6 to 6
Outputs:
- output: bfloat16 [2, 4, 1024, 1024], P(None, 'dp', 'seq')
- input_grad: bfloat16 [2, 4, 1024, 1024], P(None, 'dp', 'seq')
- attn_gain_grad: float32 [1024], P(('dp', 'seq'))
- query_weight_grad: float32 [1024, 1024], P(('dp', 'seq'))
- key_weight_grad: float32 [1024, 1024], P(('dp', 'seq'))
- value_weight_grad: float32 [1024, 1024], P(('dp', 'seq'))
- out_weight_grad: float32 [1024, 1024], P(('dp', 'seq'))
- query_gain_grad: float32 [64], replicated
- key_gain_grad: float32 [64], replicated
- variate_bias_grad: float32 [2, 16], replicated
- ffn_gain_grad: float32 [1024], P(('dp', 'seq'))
- gate_weight_grad: float32 [4096, 1024], P(('dp', 'seq'))
- up_weight_grad: float32 [4096, 1024], P(('dp', 'seq'))
- down_weight_grad: float32 [4096, 1024], P(('dp', 'seq'))
All inputs are finite; a program needn't handle non-finite values.
Results may differ from a plain program's by a relative error of at most 0.04.
Values may be sent and summed in bfloat16 or wider, within the bound.
No kernel may reach another device: no remote copies, remote signals or barrier semaphores. Data moves between devices by JAX's collectives and lax.ppermute only.
A program may use at most 256 MiB of HBM per device.

v0:
```python
import math

import jax
import jax.numpy as jnp
from jax import lax
from jax.sharding import PartitionSpec as P

D = 1024
H = 16
HD = 64
FF = 4096


epsilon = 1e-06
lowest = -1e30


def rms_scale(values):
    return lax.rsqrt(jnp.mean(values * values, axis=-1, keepdims=True) + epsilon)


def norm_back(values, inv_rms, gain_vec, upstream):
    weighted = upstream * gain_vec
    inner_mean = jnp.mean(weighted * values, axis=-1, keepdims=True)
    return inv_rms * weighted - values * (inv_rms * inv_rms * inv_rms) * inner_mean


def rotation(positions):
    half_dim = HD // 2
    frequency = 10000.0 ** (-jnp.arange(half_dim).astype(jnp.float32) / half_dim)
    angles = positions.astype(jnp.float32)[..., None] * frequency
    return (jnp.cos(angles)[..., None, :], jnp.sin(angles)[..., None, :])


def rotate(values, cos_part, sin_part):
    half_dim = values.shape[-1] // 2
    first_half = values[..., :half_dim]
    second_half = values[..., half_dim:]
    return jnp.concatenate(
        [
            first_half * cos_part - second_half * sin_part,
            first_half * sin_part + second_half * cos_part,
        ],
        axis=-1,
    )


def rotate_back(upstream, cos_part, sin_part):
    half_dim = upstream.shape[-1] // 2
    first_half = upstream[..., :half_dim]
    second_half = upstream[..., half_dim:]
    return jnp.concatenate(
        [
            first_half * cos_part + second_half * sin_part,
            second_half * cos_part - first_half * sin_part,
        ],
        axis=-1,
    )


def product(left_side, right_side):
    return jnp.dot(left_side, right_side, preferred_element_type=jnp.float32)


def times_transposed(left_side, right_side):
    return lax.dot_general(
        left_side, right_side, (((1,), (1,)), ((), ())), preferred_element_type=jnp.float32
    )


def rows_inner(left_side, right_side):
    return lax.dot_general(
        left_side, right_side, (((0,), (0,)), ((), ())), preferred_element_type=jnp.float32
    )


def score_block(queries, key_rows, query_kinds, key_kinds, variate_bias):
    raw_scores = jnp.einsum(
        "sqhe,skhe->shqk", queries, key_rows, preferred_element_type=jnp.float32
    ) * HD ** (-0.5)
    same_kind = query_kinds[:, None, :, None] == key_kinds[:, None, None, :]
    scores = raw_scores + jnp.where(
        same_kind, variate_bias[0][None, :, None, None], variate_bias[1][None, :, None, None]
    )
    return (scores, same_kind)


def forward_piece(queries, query_kinds, variate_bias, carried, pieces):
    piece_keys, piece_values, piece_kinds = pieces
    seq_count = piece_keys.shape[0]
    piece_len = piece_keys.shape[1]
    block_size = math.gcd(piece_len, 512)

    def forward_advance(block_index, totals):
        running_max, running_total, running_sum = totals
        offset = block_index * block_size
        key_rows = lax.dynamic_slice_in_dim(piece_keys, offset, block_size, 1).reshape(
            seq_count, block_size, H, HD
        )
        value_rows = lax.dynamic_slice_in_dim(piece_values, offset, block_size, 1).reshape(
            seq_count, block_size, H, HD
        )
        kind_rows = lax.dynamic_slice_in_dim(piece_kinds, offset, block_size, 1)
        scores, same_kind = score_block(queries, key_rows, query_kinds, kind_rows, variate_bias)
        new_max = jnp.maximum(running_max, jnp.max(scores, axis=-1))
        factor = jnp.exp(running_max - new_max)
        exp_scores = jnp.exp(scores - new_max[..., None])
        running_total = running_total * factor + jnp.sum(exp_scores, axis=-1)
        running_sum = running_sum * factor[..., None] + jnp.einsum(
            "shqk,skhe->shqe",
            exp_scores.astype(jnp.bfloat16),
            value_rows,
            preferred_element_type=jnp.float32,
        )
        return (new_max, running_total, running_sum)

    return lax.fori_loop(0, piece_len // block_size, forward_advance, carried)


def back_piece(context, carried, pieces):
    queries, query_kinds, grad_out, log_total, delta_row, variate_bias = context
    piece_keys, piece_values, piece_kinds = pieces
    seq_count = piece_keys.shape[0]
    piece_len = piece_keys.shape[1]
    block_size = math.gcd(piece_len, 512)
    score_scale = HD ** (-0.5)

    def back_advance(block_index, totals):
        offset = block_index * block_size
        key_rows = lax.dynamic_slice_in_dim(piece_keys, offset, block_size, 1).reshape(
            seq_count, block_size, H, HD
        )
        value_rows = lax.dynamic_slice_in_dim(piece_values, offset, block_size, 1).reshape(
            seq_count, block_size, H, HD
        )
        kind_rows = lax.dynamic_slice_in_dim(piece_kinds, offset, block_size, 1)
        scores, same_kind = score_block(queries, key_rows, query_kinds, kind_rows, variate_bias)
        attn_prob = jnp.exp(scores - log_total[..., None])
        grad_prob = jnp.einsum(
            "sqhe,skhe->shqk", grad_out, value_rows, preferred_element_type=jnp.float32
        )
        grad_score = attn_prob * (grad_prob - delta_row[..., None])
        bias_step = jnp.stack(
            [
                jnp.sum(jnp.where(same_kind, grad_score, 0.0), axis=(0, 2, 3)),
                jnp.sum(jnp.where(same_kind, 0.0, grad_score), axis=(0, 2, 3)),
            ]
        )
        score_low = grad_score.astype(jnp.bfloat16)
        query_grad = (
            totals[0]
            + jnp.einsum("shqk,skhe->shqe", score_low, key_rows, preferred_element_type=jnp.float32)
            * score_scale
        )
        key_part = (
            jnp.einsum("shqk,sqhe->skhe", score_low, queries, preferred_element_type=jnp.float32)
            * score_scale
        ).reshape(seq_count, block_size, D)
        value_part = jnp.einsum(
            "shqk,sqhe->skhe",
            attn_prob.astype(jnp.bfloat16),
            grad_out,
            preferred_element_type=jnp.float32,
        ).reshape(seq_count, block_size, D)
        key_total = lax.dynamic_update_slice_in_dim(
            totals[2],
            lax.dynamic_slice_in_dim(totals[2], offset, block_size, 1) + key_part,
            offset,
            1,
        )
        value_total = lax.dynamic_update_slice_in_dim(
            totals[3],
            lax.dynamic_slice_in_dim(totals[3], offset, block_size, 1) + value_part,
            offset,
            1,
        )
        return (query_grad, totals[1] + bias_step, key_total, value_total)

    return lax.fori_loop(0, piece_len // block_size, back_advance, carried)


def local(
    inputs,
    variate_ids,
    time_ids,
    attn_gain,
    query_weight,
    key_weight,
    value_weight,
    out_weight,
    query_gain,
    key_gain,
    variate_bias,
    ffn_gain,
    gate_weight,
    up_weight,
    down_weight,
    out_grad,
):
    seq_count = inputs.shape[1]
    tok_count = inputs.shape[2]
    row_count = seq_count * tok_count
    full_grads = [
        jnp.zeros(extent, jnp.float32)
        for extent in ((D,), (D, D), (D, D), (D, D), (D, D), (D,), (FF, D), (FF, D), (FF, D))
    ]
    small_grads = [
        jnp.zeros((HD,), jnp.float32),
        jnp.zeros((HD,), jnp.float32),
        jnp.zeros((2, H), jnp.float32),
    ]
    shard_total = None
    small_total = None
    outputs_list = []
    input_grads = []
    weights_now = None
    for micro_index in range(inputs.shape[0]):
        weights_now = (
            lax.all_gather(attn_gain.astype(jnp.bfloat16), ("dp", "seq"), axis=0, tiled=True),
            lax.all_gather(query_weight.astype(jnp.bfloat16), ("dp", "seq"), axis=0, tiled=True),
            lax.all_gather(key_weight.astype(jnp.bfloat16), ("dp", "seq"), axis=0, tiled=True),
            lax.all_gather(value_weight.astype(jnp.bfloat16), ("dp", "seq"), axis=0, tiled=True),
            lax.all_gather(out_weight.astype(jnp.bfloat16), ("dp", "seq"), axis=0, tiled=True),
            lax.all_gather(ffn_gain.astype(jnp.bfloat16), ("dp", "seq"), axis=0, tiled=True),
            lax.all_gather(gate_weight.astype(jnp.bfloat16), ("dp", "seq"), axis=0, tiled=True),
            lax.all_gather(up_weight.astype(jnp.bfloat16), ("dp", "seq"), axis=0, tiled=True),
            lax.all_gather(down_weight.astype(jnp.bfloat16), ("dp", "seq"), axis=0, tiled=True),
        )
        gain_one, w_query, w_key, w_value, w_out, gain_two, w_gate, w_up, w_down = weights_now
        hidden_in = inputs[micro_index].astype(jnp.float32).reshape(row_count, D)
        kinds_now = variate_ids[micro_index].astype(jnp.bfloat16)
        cos_part, sin_part = rotation(time_ids[micro_index])
        inv_one = rms_scale(hidden_in)
        normed = (hidden_in * inv_one * gain_one.astype(jnp.float32)).astype(jnp.bfloat16)
        query_raw = product(normed, w_query).reshape(seq_count, tok_count, H, HD)
        key_raw = product(normed, w_key).reshape(seq_count, tok_count, H, HD)
        value_flat = product(normed, w_value).astype(jnp.bfloat16).reshape(seq_count, tok_count, D)
        inv_query = rms_scale(query_raw)
        query_rot = rotate(query_raw * inv_query * query_gain, cos_part, sin_part).astype(
            jnp.bfloat16
        )
        inv_key = rms_scale(key_raw)
        key_rot = rotate(key_raw * inv_key * key_gain, cos_part, sin_part).astype(jnp.bfloat16)
        key_flat = key_rot.reshape(seq_count, tok_count, D)
        initial = (
            jnp.full((seq_count, H, tok_count), lowest, jnp.float32),
            jnp.zeros((seq_count, H, tok_count), jnp.float32),
            jnp.zeros((seq_count, H, tok_count, HD), jnp.float32),
        )
        final_max, final_total, final_sum = forward_piece(
            query_rot,
            kinds_now,
            variate_bias,
            initial,
            (
                lax.all_gather(key_flat, "seq", axis=1, tiled=True),
                lax.all_gather(value_flat, "seq", axis=1, tiled=True),
                lax.all_gather(kinds_now, "seq", axis=1, tiled=True),
            ),
        )
        log_total = final_max + jnp.log(final_total)
        attended = jnp.transpose(final_sum / final_total[..., None], (0, 2, 1, 3))
        attended_low = attended.reshape(row_count, D).astype(jnp.bfloat16)
        middle = hidden_in + product(attended_low, w_out)
        inv_two = rms_scale(middle)
        normed_two = (middle * inv_two * gain_two.astype(jnp.float32)).astype(jnp.bfloat16)
        gate_pre = times_transposed(normed_two, w_gate)
        up_pre = times_transposed(normed_two, w_up)
        gate_sig = jax.nn.sigmoid(gate_pre)
        hidden_low = (gate_pre * gate_sig * up_pre).astype(jnp.bfloat16)
        result = middle + product(hidden_low, w_down)
        outputs_list.append(result.reshape(seq_count, tok_count, D).astype(jnp.bfloat16))
        gain_one, w_query, w_key, w_value, w_out, gain_two, w_gate, w_up, w_down = (
            lax.all_gather(attn_gain.astype(jnp.bfloat16), ("dp", "seq"), axis=0, tiled=True),
            lax.all_gather(query_weight.astype(jnp.bfloat16), ("dp", "seq"), axis=0, tiled=True),
            lax.all_gather(key_weight.astype(jnp.bfloat16), ("dp", "seq"), axis=0, tiled=True),
            lax.all_gather(value_weight.astype(jnp.bfloat16), ("dp", "seq"), axis=0, tiled=True),
            lax.all_gather(out_weight.astype(jnp.bfloat16), ("dp", "seq"), axis=0, tiled=True),
            lax.all_gather(ffn_gain.astype(jnp.bfloat16), ("dp", "seq"), axis=0, tiled=True),
            lax.all_gather(gate_weight.astype(jnp.bfloat16), ("dp", "seq"), axis=0, tiled=True),
            lax.all_gather(up_weight.astype(jnp.bfloat16), ("dp", "seq"), axis=0, tiled=True),
            lax.all_gather(down_weight.astype(jnp.bfloat16), ("dp", "seq"), axis=0, tiled=True),
        )
        grad_in = out_grad[micro_index].astype(jnp.float32).reshape(row_count, D)
        grad_low = grad_in.astype(jnp.bfloat16)
        full_grads[8] = rows_inner(hidden_low, grad_low)
        grad_hidden = times_transposed(grad_low, w_down)
        grad_gate = (grad_hidden * up_pre * gate_sig * (1.0 + gate_pre * (1.0 - gate_sig))).astype(
            jnp.bfloat16
        )
        grad_up = (grad_hidden * gate_pre * gate_sig).astype(jnp.bfloat16)
        full_grads[6] = rows_inner(grad_gate, normed_two)
        full_grads[7] = rows_inner(grad_up, normed_two)
        grad_normed_two = product(grad_gate, w_gate) + product(grad_up, w_up)
        full_grads[5] = jnp.sum(grad_normed_two * middle * inv_two, axis=0)
        grad_middle = grad_in + norm_back(
            middle, inv_two, gain_two.astype(jnp.float32), grad_normed_two
        )
        grad_middle_low = grad_middle.astype(jnp.bfloat16)
        full_grads[4] = rows_inner(attended_low, grad_middle_low)
        grad_attended = (
            times_transposed(grad_middle_low, w_out)
            .astype(jnp.bfloat16)
            .reshape(seq_count, tok_count, H, HD)
        )
        delta_row = jnp.transpose(
            jnp.sum(grad_attended.astype(jnp.float32) * attended, axis=-1), (0, 2, 1)
        )
        context = (query_rot, kinds_now, grad_attended, log_total, delta_row, variate_bias)
        base_carry = (
            jnp.zeros((seq_count, H, tok_count, HD), jnp.float32),
            jnp.zeros((2, H), jnp.float32),
        )
        length_all = tok_count * lax.axis_size("seq")
        wide_carry = (
            jnp.zeros((seq_count, length_all, D), jnp.float32),
            jnp.zeros((seq_count, length_all, D), jnp.float32),
        )
        grad_query_heads, grad_bias, key_all, value_all = back_piece(
            context,
            base_carry + wide_carry,
            (
                lax.all_gather(key_flat, "seq", axis=1, tiled=True),
                lax.all_gather(value_flat, "seq", axis=1, tiled=True),
                lax.all_gather(kinds_now, "seq", axis=1, tiled=True),
            ),
        )
        grad_key, grad_value = (
            lax.psum_scatter(
                key_all.astype(jnp.bfloat16), "seq", scatter_dimension=1, tiled=True
            ).astype(jnp.float32),
            lax.psum_scatter(
                value_all.astype(jnp.bfloat16), "seq", scatter_dimension=1, tiled=True
            ).astype(jnp.float32),
        )
        grad_key = grad_key.reshape(seq_count, tok_count, H, HD)
        grad_value_low = grad_value.reshape(row_count, D).astype(jnp.bfloat16)
        small_grads[2] = grad_bias
        grad_query = jnp.transpose(grad_query_heads, (0, 2, 1, 3))
        grad_query_norm = rotate_back(grad_query, cos_part, sin_part)
        small_grads[0] = jnp.sum(grad_query_norm * query_raw * inv_query, axis=(0, 1, 2))
        grad_query_low = (
            norm_back(query_raw, inv_query, query_gain, grad_query_norm)
            .reshape(row_count, D)
            .astype(jnp.bfloat16)
        )
        grad_key_norm = rotate_back(grad_key, cos_part, sin_part)
        small_grads[1] = jnp.sum(grad_key_norm * key_raw * inv_key, axis=(0, 1, 2))
        grad_key_low = (
            norm_back(key_raw, inv_key, key_gain, grad_key_norm)
            .reshape(row_count, D)
            .astype(jnp.bfloat16)
        )
        full_grads[1] = rows_inner(normed, grad_query_low)
        full_grads[2] = rows_inner(normed, grad_key_low)
        full_grads[3] = rows_inner(normed, grad_value_low)
        grad_normed = (
            times_transposed(grad_query_low, w_query)
            + times_transposed(grad_key_low, w_key)
            + times_transposed(grad_value_low, w_value)
        )
        full_grads[0] = jnp.sum(grad_normed * hidden_in * inv_one, axis=0)
        input_total = grad_middle + norm_back(
            hidden_in, inv_one, gain_one.astype(jnp.float32), grad_normed
        )
        input_grads.append(input_total.reshape(seq_count, tok_count, D).astype(jnp.bfloat16))
        shards = (
            lax.psum_scatter(full_grads[0], ("dp", "seq"), scatter_dimension=0, tiled=True),
            lax.psum_scatter(full_grads[1], ("dp", "seq"), scatter_dimension=0, tiled=True),
            lax.psum_scatter(full_grads[2], ("dp", "seq"), scatter_dimension=0, tiled=True),
            lax.psum_scatter(full_grads[3], ("dp", "seq"), scatter_dimension=0, tiled=True),
            lax.psum_scatter(full_grads[4], ("dp", "seq"), scatter_dimension=0, tiled=True),
            lax.psum_scatter(full_grads[5], ("dp", "seq"), scatter_dimension=0, tiled=True),
            lax.psum_scatter(full_grads[6], ("dp", "seq"), scatter_dimension=0, tiled=True),
            lax.psum_scatter(full_grads[7], ("dp", "seq"), scatter_dimension=0, tiled=True),
            lax.psum_scatter(full_grads[8], ("dp", "seq"), scatter_dimension=0, tiled=True),
        )
        summed = lax.psum((small_grads[0], small_grads[1], small_grads[2]), ("dp", "seq"))
        shards, summed = (list(shards), list(summed))
        if shard_total is None:
            shard_total = shards
            small_total = summed
        else:
            shard_total = [
                earlier_part + later_part for earlier_part, later_part in zip(shard_total, shards)
            ]
            small_total = [
                earlier_part + later_part for earlier_part, later_part in zip(small_total, summed)
            ]
        full_grads = [jnp.zeros_like(member) for member in full_grads]
        small_grads = [jnp.zeros_like(member) for member in small_grads]
    return (
        jnp.stack(outputs_list),
        jnp.stack(input_grads),
        shard_total[0],
        shard_total[1],
        shard_total[2],
        shard_total[3],
        shard_total[4],
        small_total[0],
        small_total[1],
        small_total[2],
        shard_total[5],
        shard_total[6],
        shard_total[7],
        shard_total[8],
    )


def solution(mesh):
    placed = (
        P(None, "dp", "seq", None),
        P(None, "dp", "seq"),
        P(None, "dp", "seq"),
        P(("dp", "seq")),
        P(("dp", "seq"), None),
        P(("dp", "seq"), None),
        P(("dp", "seq"), None),
        P(("dp", "seq"), None),
        P(),
        P(),
        P(),
        P(("dp", "seq")),
        P(("dp", "seq"), None),
        P(("dp", "seq"), None),
        P(("dp", "seq"), None),
        P(None, "dp", "seq", None),
    )
    return jax.shard_map(
        local,
        mesh=mesh,
        in_specs=placed,
        out_specs=(
            P(None, "dp", "seq", None),
            P(None, "dp", "seq", None),
            P(("dp", "seq")),
            P(("dp", "seq"), None),
            P(("dp", "seq"), None),
            P(("dp", "seq"), None),
            P(("dp", "seq"), None),
            P(),
            P(),
            P(),
            P(("dp", "seq")),
            P(("dp", "seq"), None),
            P(("dp", "seq"), None),
            P(("dp", "seq"), None),
        ),
        check_vma=False,
    )
```

profile of v0, /device:TPU:0, one launch (start us, length us, event | category | flops | bytes accessed | tf_op | source)
XLA Modules:
  0.0 2017.1 jit_solution(1738610044664520707)
XLA Ops:
  13.9 42.1 %all-reduce.5 = (bf16[1024]{0:T(1024)(128)(2,1)S(1)}, bf16[1024]{0:T(1024)(128)(2,1)S(1)}) all-reduce(bf16[1024]{0:T(1024)(128)(2,1)S(1)} %dynamic-update-slice, bf16[1024]{0:T(1024)(128)(2,1)S(1)} %dynamic-update-slice.1), channel_id=1, replica_groups=mesh['dp'=4,'seq'=8] {'dp','seq'}, use_global_device_ids=true, to_apply=%add | all-reduce | flops 2048 | bytes 8192
  57.7 13.1 all-gather.22.cloned.1.call-done
  76.9 52.8 %all-gather.20.cloned.1.call-done = bf16[1024,1024]{1,0:T(8,128)(2,1)} async-done(((bf16[32,1024]{1,0:T(8,128)(2,1)}), bf16[1024,1024]{1,0:T(8,128)(2,1)}) %all-gather.20.cloned.1.call-update) | async-done | bytes 2097168 | tf_op jit(solution)/shard_map/all_gather | solution.py:220
  136.3 52.4 %all-gather.16.cloned.1.call-done = bf16[1024,1024]{1,0:T(8,128)(2,1)} async-done(((bf16[32,1024]{1,0:T(8,128)(2,1)}), bf16[1024,1024]{1,0:T(8,128)(2,1)}) %all-gather.16.cloned.1.call-update) | async-done | bytes 2097168 | tf_op jit(solution)/shard_map/all_gather | solution.py:221
  210.8 10.5 all-gather.2
  221.2 8.8 all-gather
  233.0 15.2 all-gather.34.cloned.1.call-done
  252.1 27.9 %all-gather.18.cloned.1.call-done = bf16[1,1024,1024]{1,2,0:T(8,128)(2,1)} async-done(((bf16[1,128,1024]{1,2,0:T(8,128)(2,1)}), bf16[1,1024,1024]{1,2,0:T(8,128)(2,1)}) %all-gather.18.cloned.1.call-update) | async-done | bytes 2097168 | tf_op jit(solution)/shard_map/all_gather | solution.py:256
  280.0 26.8 %while.76 = (s32[]{:T(128)}, f32[1,16,128]{2,1,0:T(8,128)S(1)}, f32[1,16,128]{2,1,0:T(8,128)S(1)}, f32[1,16,128,64]{2,3,1,0:T(8,128)}, bf16[1,1024,1024]{1,2,0:T...) while((s32[]{:T(128)}, f32[1,16,128]{2,1,0:T(8,128)S(1)}, ...), condition=%wide.region_6.7_spmd.clone, body=%wide.region_3.6_spmd.clone.sunk | while | flops 283586560 | bytes 37359720 | solution.py:117
  308.0 31.2 %all-gather.24.cloned.1.call-done = bf16[1024,1024]{1,0:T(8,128)(2,1)} async-done(((bf16[32,1024]{1,0:T(8,128)(2,1)}), bf16[1024,1024]{1,0:T(8,128)(2,1)}) %all-gather.24.cloned.1.call-update) | async-done | bytes 2097168 | tf_op jit(solution)/shard_map/all_gather | solution.py:223
  342.0 28.4 %all-gather.32.cloned.1.call-done = bf16[1,1024,1024]{1,2,0:T(8,128)(2,1)} async-done(((bf16[1,128,1024]{1,2,0:T(8,128)(2,1)}), bf16[1,1024,1024]{1,2,0:T(8,128)(2,1)}) %all-gather.32.cloned.1.call-update) | async-done | bytes 2097168 | tf_op jit(solution)/shard_map/all_gather | solution.py:256
  370.5 26.7 %while.77 = (s32[]{:T(128)}, f32[1,16,128]{2,1,0:T(8,128)S(1)}, f32[1,16,128]{2,1,0:T(8,128)S(1)}, f32[1,16,128,64]{2,3,1,0:T(8,128)}, bf16[1,1024,1024]{1,2,0:T...) while((s32[]{:T(128)}, f32[1,16,128]{2,1,0:T(8,128)S(1)}, ...), condition=%wide.region_14.15_spmd.clone, body=%wide.region_11.14_spmd.clone.sunk | while | flops 283586560 | bytes 37359720 | solution.py:117
  401.9 48.1 %all-gather.26.cloned.1.call-done = bf16[4096,1024]{1,0:T(8,128)(2,1)} async-done(((bf16[128,1024]{1,0:T(8,128)(2,1)}), bf16[4096,1024]{1,0:T(8,128)(2,1)}) %all-gather.26.cloned.1.call-update) | async-done | bytes 8388624 | tf_op jit(solution)/shard_map/all_gather | solution.py:225
  457.6 71.1 %all-gather.28.cloned.1.call-done = bf16[4096,1024]{1,0:T(8,128)(2,1)} async-done(((bf16[128,1024]{1,0:T(8,128)(2,1)}), bf16[4096,1024]{1,0:T(8,128)(2,1)}) %all-gather.28.cloned.1.call-update) | async-done | bytes 8388624 | tf_op jit(solution)/shard_map/all_gather | solution.py:226
  536.3 71.5 %all-gather.30.cloned.1.call-done = bf16[4096,1024]{1,0:T(8,128)(2,1)} async-done(((bf16[128,1024]{1,0:T(8,128)(2,1)}), bf16[4096,1024]{1,0:T(8,128)(2,1)}) %all-gather.30.cloned.1.call-update) | async-done | bytes 8388624 | tf_op jit(solution)/shard_map/all_gather | solution.py:227
  607.7 8.9 multiply_convert_fusion.2
  634.9 8.9 multiply_convert_fusion
  655.4 38.9 %while.78 = (s32[]{:T(128)}, f32[1,16,128,64]{2,3,1,0:T(8,128)}, f32[2,16]{1,0:T(2,128)S(1)}, f32[1,1024,1024]{1,2,0:T(8,128)}, f32[1,1024,1024]{1,2,0:T(8,128)}...) while((s32[]{:T(128)}, f32[1,16,128,64]{2,3,1,0:T(8,128)}, ...), condition=%wide.region_21.22_spmd.clone, body=%wide.region_18.21_spmd.clone.sunk | while | flops 689897536 | bytes 150172448 | solution.py:179
  717.1 38.6 %while.79 = (s32[]{:T(128)}, f32[1,16,128,64]{2,3,1,0:T(8,128)}, f32[2,16]{1,0:T(2,128)S(1)}, f32[1,1024,1024]{1,2,0:T(8,128)}, f32[1,1024,1024]{1,2,0:T(8,128)}...) while((s32[]{:T(128)}, f32[1,16,128,64]{2,3,1,0:T(8,128)}, ...), condition=%wide.region_32.33_spmd.clone, body=%wide.region_29.32_spmd.clone.sunk | while | flops 689897536 | bytes 148075232 | solution.py:179
  758.2 7.8 copy.208
  851.0 27.2 %reduce-scatter.36.cloned.1.call-done = bf16[128,1024]{1,0:T(8,128)(2,1)} async-done(((bf16[1024,1024]{1,0:T(8,128)(2,1)}), bf16[128,1024]{1,0:T(8,128)(2,1)}) %reduce-scatter.36.cloned.1.call-update) | async-done | bytes 262160
  887.2 8.2 convolution_add_fusion.2
  899.1 8.2 convolution_add_fusion.1
  911.9 8.2 convolution_add_fusion
  939.0 38.4 %all-reduce.4 = (f32[1024]{0:T(1024)S(1)}, f32[64]{0:T(128)}, f32[64]{0:T(128)}, f32[2,16]{1,0:T(2,128)}, f32[1024]{0:T(1024)S(1)}) all-reduce(f32[1024]{0:T(1024)S(1)} %add.536, f32[64]{0:T(128)S(1)} %add.529, f32[64]{0:T(128)S(1)} %add.530, f32[2,16]{1,0:T(2,128)S(1)} %add.531, ...), channel_id=19, replica_groups=mesh['dp'=4,'seq'=8] {'dp','seq'}, use_global_device_ids=true, to_apply=%region_39.40.clone | all-reduce | flops 2208 | bytes 17664
  979.8 42.4 %reduce-scatter.26.cloned.1.call-done = f32[32,1024]{1,0:T(8,128)} async-done(((f32[1024,1024]{1,0:T(8,128)}), f32[32,1024]{1,0:T(8,128)}) %reduce-scatter.26.cloned.1.call-update) | async-done | bytes 131088 | tf_op jit(solution)/shard_map/reduce_scatter | solution.py:372
  1022.2 142.0 %reduce-scatter.20.cloned.1.call-done = f32[32,1024]{1,0:T(8,128)} async-done(((f32[1024,1024]{1,0:T(8,128)}), f32[32,1024]{1,0:T(8,128)}) %reduce-scatter.20.cloned.1.call-update) | async-done | bytes 131088 | tf_op jit(solution)/shard_map/reduce_scatter | solution.py:369
  1164.2 142.3 %reduce-scatter.22.cloned.1.call-done = f32[32,1024]{1,0:T(8,128)} async-done(((f32[1024,1024]{1,0:T(8,128)}), f32[32,1024]{1,0:T(8,128)}) %reduce-scatter.22.cloned.1.call-update) | async-done | bytes 131088 | tf_op jit(solution)/shard_map/reduce_scatter | solution.py:370
  1306.5 142.5 %reduce-scatter.24.cloned.1.call-done = f32[32,1024]{1,0:T(8,128)} async-done(((f32[1024,1024]{1,0:T(8,128)}), f32[32,1024]{1,0:T(8,128)}) %reduce-scatter.24.cloned.1.call-update) | async-done | bytes 131088 | tf_op jit(solution)/shard_map/reduce_scatter | solution.py:371
  1449.0 186.3 %reduce-scatter.28.cloned.1.call-done = f32[128,1024]{1,0:T(8,128)} async-done(((f32[4096,1024]{1,0:T(8,128)}), f32[128,1024]{1,0:T(8,128)}) %reduce-scatter.28.cloned.1.call-update) | async-done | bytes 524304 | tf_op jit(solution)/shard_map/reduce_scatter | solution.py:374
  1635.3 187.3 %reduce-scatter.30.cloned.1.call-done = f32[128,1024]{1,0:T(8,128)} async-done(((f32[4096,1024]{1,0:T(8,128)}), f32[128,1024]{1,0:T(8,128)}) %reduce-scatter.30.cloned.1.call-update) | async-done | bytes 524304 | tf_op jit(solution)/shard_map/reduce_scatter | solution.py:375
  1822.5 187.3 %reduce-scatter.32.cloned.1.call-done = f32[128,1024]{1,0:T(8,128)} async-done(((f32[4096,1024]{1,0:T(8,128)}), f32[128,1024]{1,0:T(8,128)}) %reduce-scatter.32.cloned.1.call-update) | async-done | bytes 524304 | tf_op jit(solution)/shard_map/reduce_scatter | solution.py:376
  (641 shorter events, 380.3 us)
Async XLA Ops:
  7.2 66.6 %copy-start.16 = (bf16[2,1,128,1024]{3,2,1,0:T(8,128)(2,1)S(1)}, bf16[2,1,128,1024]{3,2,1,0:T(8,128)(2,1)}, u32[]{:S(2)}) copy-start(bf16[2,1,128,1024]{3,2,1,0:T(8,128)(2,1)} %param.24) | copy-start | bytes 1572868
  7.2 63.6 %all-gather.22.cloned.1.call-start = ((), (), s32[]{:S(2)}) async-start(), calls=%async_computation.14 | async-start | bytes 2162688 | tf_op jit(solution)/shard_map/all_gather | solution.py:222
  8.9 120.9 %all-gather.20.cloned.1.call-start = ((), (), s32[]{:S(2)}) async-start(), calls=%async_computation.13 | async-start | bytes 2162688 | tf_op jit(solution)/shard_map/all_gather | solution.py:220
  10.5 178.2 %all-gather.16.cloned.1.call-start = ((), (), s32[]{:S(2)}) async-start(), calls=%async_computation.11 | async-start | bytes 2162688 | tf_op jit(solution)/shard_map/all_gather | solution.py:221
  12.1 218.0 %all-gather.36.cloned.1.call-start = ((), (), s32[]{:S(2)}) async-start(), calls=%async_computation.21 | async-start | bytes 2359296 | tf_op jit(solution)/shard_map/all_gather | solution.py:257
  55.9 137.1 %copy-start.92 = (f32[1024]{0:T(1024)}, f32[1024]{0:T(1024)S(1)}, u32[]{:S(2)}) copy-start(f32[1024]{0:T(1024)S(1)} %convert_element_type.403) | copy-start | bytes 12292
  57.7 131.0 %copy-start.114 = (f32[128]{0:T(128)}, f32[128]{0:T(128)S(1)}, u32[]{:S(2)}) copy-start(f32[128]{0:T(128)S(1)} %get-tuple-element.1417) | copy-start | bytes 1540
  57.7 135.3 %copy-start.112 = (f32[128]{0:T(128)}, f32[128]{0:T(128)S(1)}, u32[]{:S(2)}) copy-start(f32[128]{0:T(128)S(1)} %get-tuple-element.1399) | copy-start | bytes 1540
  73.7 174.5 %all-gather.34.cloned.1.call-start = ((), (), s32[]{:S(2)}) async-start(), calls=%async_computation.20 | async-start | bytes 2359296 | tf_op jit(solution)/shard_map/all_gather | solution.py:257
  76.6 203.4 %all-gather.18.cloned.1.call-start = ((), (), s32[]{:S(2)}) async-start(), calls=%async_computation.12 | async-start | bytes 2359296 | tf_op jit(solution)/shard_map/all_gather | solution.py:256
  76.9 125.4 %copy-start.99 = (f32[128,32]{0,1:T(8,128)}, f32[128,32]{0,1:T(8,128)S(1)}, u32[]{:S(2)}) copy-start(f32[128,32]{0,1:T(8,128)S(1)} %get-tuple-element.1390) | copy-start | bytes 49156
  76.9 125.4 %copy-start.101 = (f32[128,32]{0,1:T(8,128)}, f32[128,32]{0,1:T(8,128)S(1)}, u32[]{:S(2)}) copy-start(f32[128,32]{0,1:T(8,128)S(1)} %get-tuple-element.1391) | copy-start | bytes 49156
  76.9 127.1 %copy-start.95 = (f32[128,32]{0,1:T(8,128)}, f32[128,32]{0,1:T(8,128)S(1)}, u32[]{:S(2)}) copy-start(f32[128,32]{0,1:T(8,128)S(1)} %get-tuple-element.1406) | copy-start | bytes 49156
  76.9 127.1 %copy-start.97 = (f32[128,32]{0,1:T(8,128)}, f32[128,32]{0,1:T(8,128)S(1)}, u32[]{:S(2)}) copy-start(f32[128,32]{0,1:T(8,128)S(1)} %get-tuple-element.1407) | copy-start | bytes 49156
  203.3 135.9 %all-gather.24.cloned.1.call-start = ((), (), s32[]{:S(2)}) async-start(), calls=%async_computation.15 | async-start | bytes 2162688 | tf_op jit(solution)/shard_map/all_gather | solution.py:223
  204.0 166.4 %all-gather.32.cloned.1.call-start = ((), (), s32[]{:S(2)}) async-start(), calls=%async_computation.19 | async-start | bytes 2359296 | tf_op jit(solution)/shard_map/all_gather | solution.py:256
  205.0 245.0 %all-gather.26.cloned.1.call-start = ((), (), s32[]{:S(2)}) async-start(), calls=%async_computation.16 | async-start | bytes 8650752 | tf_op jit(solution)/shard_map/all_gather | solution.py:225
  206.9 321.8 %all-gather.28.cloned.1.call-start = ((), (), s32[]{:S(2)}) async-start(), calls=%async_computation.17 | async-start | bytes 8650752 | tf_op jit(solution)/shard_map/all_gather | solution.py:226
  208.7 399.0 %all-gather.30.cloned.1.call-start = ((), (), s32[]{:S(2)}) async-start(), calls=%async_computation.18 | async-start | bytes 8650752 | tf_op jit(solution)/shard_map/all_gather | solution.py:227
  210.6 598.1 %reduce-scatter.34.cloned.1.call-start = ((), (), s32[]{:S(2)}) async-start(), calls=%async_computation.29 | async-start | bytes 2359296
  401.9 126.8 %copy-start.56 = (bf16[128,1024]{1,0:T(8,128)(2,1)}, bf16[128,1024]{1,0:T(8,128)(2,1)S(1)}, u32[]{:S(2)}) copy-start(bf16[128,1024]{1,0:T(8,128)(2,1)S(1)} %multiply_convert_fusion.7) | copy-start | bytes 786436
  457.6 150.1 %copy-start.81 = (bf16[2,1,128,1024]{3,2,1,0:T(8,128)(2,1)S(1)}, bf16[2,1,128,1024]{3,2,1,0:T(8,128)(2,1)}, u32[]{:S(2)}) copy-start(bf16[2,1,128,1024]{3,2,1,0:T(8,128)(2,1)} %param.39) | copy-start | bytes 1572868
  709.1 102.1 %reduce-scatter.38.cloned.1.call-start = ((), (), s32[]{:S(2)}) async-start(), calls=%async_computation.31 | async-start | bytes 2359296
  770.3 79.0 %reduce-scatter.40.cloned.1.call-start = ((), (), s32[]{:S(2)}) async-start(), calls=%async_computation.32 | async-start | bytes 2359296
  785.1 93.1 %reduce-scatter.36.cloned.1.call-start = ((), (), s32[]{:S(2)}) async-start(), calls=%async_computation.30 | async-start | bytes 2359296
  799.9 222.4 %reduce-scatter.26.cloned.1.call-start = ((), (), s32[]{:S(2)}) async-start(), calls=%async_computation.25 | async-start | bytes 4325376 | tf_op jit(solution)/shard_map/reduce_scatter | solution.py:372
  803.8 360.5 %reduce-scatter.20.cloned.1.call-start = ((), (), s32[]{:S(2)}) async-start(), calls=%async_computation.22 | async-start | bytes 4325376 | tf_op jit(solution)/shard_map/reduce_scatter | solution.py:369
  829.3 477.1 %reduce-scatter.22.cloned.1.call-start = ((), (), s32[]{:S(2)}) async-start(), calls=%async_computation.23 | async-start | bytes 4325376 | tf_op jit(solution)/shard_map/reduce_scatter | solution.py:370
  849.2 599.8 %reduce-scatter.24.cloned.1.call-start = ((), (), s32[]{:S(2)}) async-start(), calls=%async_computation.24 | async-start | bytes 4325376 | tf_op jit(solution)/shard_map/reduce_scatter | solution.py:371
  883.6 751.7 %reduce-scatter.28.cloned.1.call-start = ((), (), s32[]{:S(2)}) async-start(), calls=%async_computation.26 | async-start | bytes 17301504 | tf_op jit(solution)/shard_map/reduce_scatter | solution.py:374
  895.5 927.0 %reduce-scatter.30.cloned.1.call-start = ((), (), s32[]{:S(2)}) async-start(), calls=%async_computation.27 | async-start | bytes 17301504 | tf_op jit(solution)/shard_map/reduce_scatter | solution.py:375
  907.3 1102.5 %reduce-scatter.32.cloned.1.call-start = ((), (), s32[]{:S(2)}) async-start(), calls=%async_computation.28 | async-start | bytes 17301504 | tf_op jit(solution)/shard_map/reduce_scatter | solution.py:376
  (145 other events, 990.0 us)
Sparse Core Ops, SparseCore 0:
  11.6 59.1 all-gather.21
  74.4 55.3 all-gather.19
  133.3 55.3 all-gather.15
  190.1 27.9 all-gather.35
  219.6 28.5 all-gather.33
  249.7 30.3 all-gather.17
  283.6 55.5 all-gather.23
  340.7 29.6 all-gather.31
  373.5 76.4 all-gather.25
  452.8 75.8 all-gather.27
  531.7 75.9 all-gather.29
  709.2 34.3 reduce-scatter.33
  770.5 34.3 reduce-scatter.37
  807.0 34.4 reduce-scatter.39
  843.6 34.5 reduce-scatter.35
  880.9 141.2 reduce-scatter.25
  1024.9 139.2 reduce-scatter.19
  1166.9 139.5 reduce-scatter.21
  1309.3 139.6 reduce-scatter.23
  1451.7 183.4 reduce-scatter.27
  1638.1 184.3 reduce-scatter.29
  1825.4 184.3 reduce-scatter.31
where the time goes:
time: 2020 us
  waiting for transfers between devices  1470 us (73%)
  matrix products  209 us (10%)
  local copies, waits for them, and re-layouts  146 us (7%)
  blocking collectives  99.8 us (5%)
  other arithmetic  73.1 us (4%)
    reduce_scatter x1, waiting for transfers between devices, local(): lax.psum_scatter(full_grads[8], ('dp', 'seq'), scatter_dimension=0, tiled...  187 us
    reduce_scatter x1, waiting for transfers between devices, local(): lax.psum_scatter(full_grads[7], ('dp', 'seq'), scatter_dimension=0, tiled...  187 us
    reduce_scatter x1, waiting for transfers between devices, local(): lax.psum_scatter(full_grads[6], ('dp', 'seq'), scatter_dimension=0, tiled...  186 us
    reduce_scatter x1, waiting for transfers between devices, local(): lax.psum_scatter(full_grads[3], ('dp', 'seq'), scatter_dimension=0, tiled...  143 us
    reduce_scatter x1, waiting for transfers between devices, local(): lax.psum_scatter(full_grads[2], ('dp', 'seq'), scatter_dimension=0, tiled...  142 us
    reduce_scatter x1, waiting for transfers between devices, local(): lax.psum_scatter(full_grads[1], ('dp', 'seq'), scatter_dimension=0, tiled...  142 us
    unnamed x2, blocking collectives  80.5 us
    all_gather x1, waiting for transfers between devices, local(): lax.all_gather(down_weight.astype(jnp.bfloat16), ('dp', 'seq'), axis=0, t...  71.5 us
  transfers between devices with their start and end apart: 22, of which 18 were waited for; matrix products, arithmetic and copies ran while one was open for 15% of the time, Pallas kernels for 0%

commit v1 on v0

--- a/solution.py
+++ b/solution.py
@@ -3,6 +3,8 @@
 import jax
 import jax.numpy as jnp
 from jax import lax
+from jax.experimental import pallas as pl
+from jax.experimental.pallas import tpu as pltpu
 from jax.sharding import PartitionSpec as P
 
 D = 1024
@@ -407,6 +409,603 @@
     )
 
 
+def swap_seq(values, mask):
+    return lax.ppermute(values, "seq", [(at, at ^ mask) for at in range(8)])
+
+
+def swap_dp(values, mask):
+    return lax.ppermute(values, "dp", [(at, at ^ mask) for at in range(4)])
+
+
+def pick(pieces, which):
+    chosen = pieces[-1]
+    for at in range(len(pieces) - 2, -1, -1):
+        chosen = jnp.where(which == at, pieces[at], chosen)
+    return chosen
+
+
+def ordered(pieces, own):
+    return jnp.stack([pick(pieces, own ^ at) for at in range(len(pieces))])
+
+
+def at_index(values, index, axis=0):
+    return lax.dynamic_index_in_dim(values, index, axis, keepdims=False)
+
+
+def contract_last(left_side, right_side):
+    return lax.dot_general(
+        left_side, right_side, (((1,), (1,)), ((), ())), preferred_element_type=jnp.float32
+    )
+
+
+def exact(left_side, right_side):
+    return jnp.dot(
+        left_side,
+        right_side,
+        precision=lax.Precision.HIGHEST,
+        preferred_element_type=jnp.float32,
+    )
+
+
+def head_block(scale):
+    rows = lax.broadcasted_iota(jnp.int32, (128, 128), 0) // HD
+    columns = lax.broadcasted_iota(jnp.int32, (128, 128), 1) // HD
+    return jnp.where(rows == columns, scale, 0.0).astype(jnp.float32)
+
+
+def rope_partner(values):
+    lane = lax.broadcasted_iota(jnp.int32, values.shape, 1)
+    return jnp.where(
+        lane % HD < HD // 2, pltpu.roll(values, 128 - HD // 2, 1), pltpu.roll(values, HD // 2, 1)
+    )
+
+
+def three_parts(values):
+    first = values.astype(jnp.bfloat16).astype(jnp.float32)
+    second = (values - first).astype(jnp.bfloat16).astype(jnp.float32)
+    third = (values - first - second).astype(jnp.bfloat16).astype(jnp.float32)
+    return first, second, third
+
+
+BQ = 256
+BK = 256
+LSE_LANE = 24
+
+
+def attend_kernel(
+    q_in,
+    k_in,
+    v_in,
+    cos_in,
+    sin_in,
+    hot_in,
+    q_gain,
+    k_gain,
+    bias_in,
+    att_out,
+    qs_out,
+    ks_out,
+    vs_out,
+    ext_out,
+    kx,
+    vx,
+):
+    mean_block = head_block(1.0 / HD)
+
+    def prepare(raw, gain):
+        inv = lax.rsqrt(exact(raw * raw, mean_block) + epsilon)
+        scaled = raw * inv * gain
+        return scaled * cos_in[...] + rope_partner(scaled) * sin_in[...]
+
+    qs_out[...] = (
+        prepare(q_in[...], q_gain[...]).astype(jnp.bfloat16).astype(jnp.float32) * HD**-0.5
+    ).astype(jnp.bfloat16)
+    keys = prepare(k_in[...], k_gain[...]).astype(jnp.bfloat16)
+    ks_out[...] = keys
+    kx[:, :128] = keys
+    kx[:, 128:] = hot_in[...]
+    values = v_in[...].astype(jnp.bfloat16)
+    vs_out[...] = values
+    vx[:, :128] = values
+    vx[:, 128:] = jnp.ones(values.shape, jnp.bfloat16)
+    lane = lax.broadcasted_iota(jnp.int32, (BQ, 128), 1)
+
+    def step(block, carry):
+        rows = pl.ds(pl.multiple_of(block * BQ, BQ), BQ)
+        queries = qs_out[rows, :].astype(jnp.float32)
+        hot = hot_in[rows, :].astype(jnp.float32)
+        results = []
+        for head in range(2):
+            mine = jnp.where(lane // HD == head, queries, 0.0).astype(jnp.bfloat16)
+            extra = hot * bias_in[0, head : head + 1, :]
+            scores = contract_last(
+                jnp.concatenate([mine, extra.astype(jnp.bfloat16)], axis=1), kx[...]
+            )
+            weights = jnp.exp(scores).astype(jnp.bfloat16)
+            summed = jnp.dot(weights, vx[...], preferred_element_type=jnp.float32)
+            total = summed[:, 128:]
+            results.append(summed[:, :128] / total)
+            first, second, third = three_parts(-jnp.log(total))
+            extra = jnp.where(lane == LSE_LANE, first, extra)
+            extra = jnp.where(lane == LSE_LANE + 1, second, extra)
+            extra = jnp.where(lane == LSE_LANE + 2, third, extra)
+            ext_out[head, rows, :] = extra.astype(jnp.bfloat16)
+        att_out[rows, :] = jnp.where(lane < HD, results[0], results[1]).astype(jnp.bfloat16)
+        return carry
+
+    lax.fori_loop(0, q_in.shape[0] // BQ, step, 0)
+
+
+def attend_back_kernel(
+    q_in,
+    k_in,
+    qs_in,
+    ks_in,
+    vs_in,
+    ext_in,
+    hot_in,
+    grad_in,
+    att_in,
+    cos_in,
+    sin_in,
+    q_gain,
+    k_gain,
+    dq_out,
+    dk_out,
+    dv_out,
+    gain_out,
+    bias_out,
+    kx,
+    vx,
+    kt,
+    qx,
+    qg,
+    gx,
+    dqt,
+    dk_sum,
+    dv_sum,
+):
+    tokens = q_in.shape[0]
+    lane = lax.broadcasted_iota(jnp.int32, (tokens, 128), 1)
+    keys = ks_in[...]
+    kx[:, :128] = keys
+    kx[:, 128:] = hot_in[...]
+    kt[...] = keys.astype(jnp.float32).T.astype(jnp.bfloat16)
+    vx[:, :128] = vs_in[...]
+    vx[:, 128:] = jnp.where(lane % HD < 3, 1.0, 0.0).astype(jnp.bfloat16)
+    grads = grad_in[...].astype(jnp.float32)
+    delta = exact(grads * att_in[...].astype(jnp.float32), head_block(1.0))
+    first, second, third = three_parts(-delta)
+    parts = jnp.where(
+        lane % HD == 0,
+        first,
+        jnp.where(lane % HD == 1, second, jnp.where(lane % HD == 2, third, 0.0)),
+    )
+    queries = qs_in[...].astype(jnp.float32)
+    for head in range(2):
+        own = lane // HD == head
+        mine = jnp.where(own, queries, 0.0).astype(jnp.bfloat16)
+        qx[head, :, :128] = mine
+        qx[head, :, 128:] = ext_in[head]
+        qg[head, :, :128] = mine
+        qg[head, :, 128:] = hot_in[...]
+        gx[head, :, :128] = jnp.where(own, grads, 0.0).astype(jnp.bfloat16)
+        gx[head, :, 128:] = jnp.where(own, parts, 0.0).astype(jnp.bfloat16)
+    dqt[...] = jnp.zeros(dqt.shape, jnp.float32)
+    block_lane = lax.broadcasted_iota(jnp.int32, (BK, 128), 1)
+    counted = jnp.where((block_lane < 8) | (block_lane == LSE_LANE), 1.0, 0.0)
+
+    def step(block, carry):
+        rows = pl.ds(pl.multiple_of(block * BK, BK), BK)
+        hot = hot_in[rows, :].astype(jnp.float32) * counted
+        dk_parts = []
+        dv_parts = []
+        bias_parts = []
+        for head in range(2):
+            probs = jnp.exp(contract_last(kx[rows, :], qx[head]))
+            dscores = (probs * contract_last(vx[rows, :], gx[head])).astype(jnp.bfloat16)
+            dv_parts.append(
+                jnp.dot(
+                    probs.astype(jnp.bfloat16), gx[head, :, :128], preferred_element_type=jnp.float32
+                )
+            )
+            wide = jnp.dot(dscores, qg[head], preferred_element_type=jnp.float32)
+            dk_parts.append(wide[:, :128])
+            bias_parts.append(jnp.sum(wide[:, 128:] * hot, axis=0, keepdims=True))
+            head_rows = pl.ds(head * HD, HD)
+            dqt[head_rows, :] += jnp.dot(
+                kt[head_rows, rows], dscores, preferred_element_type=jnp.float32
+            )
+        dk_sum[rows, :] = dk_parts[0] + dk_parts[1]
+        dv_sum[rows, :] = dv_parts[0] + dv_parts[1]
+        return (carry[0] + bias_parts[0], carry[1] + bias_parts[1])
+
+    zero = jnp.zeros((1, 128), jnp.float32)
+    sums = lax.fori_loop(0, tokens // BK, step, (zero, zero))
+    bias_out[0, 0:1, :] = sums[0]
+    bias_out[0, 1:2, :] = sums[1]
+    mean_block = head_block(1.0 / HD)
+
+    def finish(raw, upstream, gain):
+        inv = lax.rsqrt(exact(raw * raw, mean_block) + epsilon)
+        normed = upstream * cos_in[...] - rope_partner(upstream) * sin_in[...]
+        gain_grad = jnp.sum(normed * raw * inv, axis=0, keepdims=True)
+        weighted = normed * gain
+        inner = exact(weighted * raw, mean_block)
+        return inv * weighted - raw * (inv * inv * inv) * inner, gain_grad
+
+    dq, dq_gain = finish(q_in[...], dqt[...].T * HD**-0.5, q_gain[...])
+    dk, dk_gain = finish(k_in[...], dk_sum[...], k_gain[...])
+    dq_out[...] = dq.astype(jnp.bfloat16)
+    dk_out[...] = dk.astype(jnp.bfloat16)
+    dv_out[...] = dv_sum[...].astype(jnp.bfloat16)
+    gain_out[0, 0:1, :] = dq_gain
+    gain_out[0, 1:2, :] = dk_gain
+
+
+def attend(qkv, cos_part, sin_part, hot, q_gain, k_gain, bias_rows):
+    tokens = qkv.shape[0]
+    column = lambda shift: pl.BlockSpec((tokens, 128), lambda pair: (0, pair + shift))
+    whole = pl.BlockSpec((tokens, 128), lambda pair: (0, 0))
+    line = pl.BlockSpec((1, 128), lambda pair: (0, 0))
+    low = lambda: jax.ShapeDtypeStruct((tokens, 256), jnp.bfloat16)
+    return pl.pallas_call(
+        attend_kernel,
+        grid=(2,),
+        in_specs=[
+            column(0),
+            column(2),
+            column(4),
+            whole,
+            whole,
+            whole,
+            line,
+            line,
+            pl.BlockSpec((1, 2, 128), lambda pair: (pair, 0, 0)),
+        ],
+        out_specs=[
+            column(0),
+            column(0),
+            column(0),
+            column(0),
+            pl.BlockSpec((2, tokens, 128), lambda pair: (pair, 0, 0)),
+        ],
+        out_shape=[
+            low(),
+            low(),
+            low(),
+            low(),
+            jax.ShapeDtypeStruct((4, tokens, 128), jnp.bfloat16),
+        ],
+        scratch_shapes=[
+            pltpu.VMEM((tokens, 256), jnp.bfloat16),
+            pltpu.VMEM((tokens, 256), jnp.bfloat16),
+        ],
+        compiler_params=pltpu.CompilerParams(vmem_limit_bytes=40 << 20),
+        cost_estimate=pl.CostEstimate(
+            flops=16 * tokens * tokens * 256,
+            bytes_accessed=tokens * 256 * 30,
+            transcendentals=4 * tokens * tokens,
+        ),
+        name="attend",
+    )(qkv, qkv, qkv, cos_part, sin_part, hot, q_gain, k_gain, bias_rows)
+
+
+def attend_back(qkv, saved, hot, grads, attended, cos_part, sin_part, q_gain, k_gain):
+    queries, keys, values, extra = saved
+    tokens = qkv.shape[0]
+    column = lambda shift: pl.BlockSpec((tokens, 128), lambda pair: (0, pair + shift))
+    whole = pl.BlockSpec((tokens, 128), lambda pair: (0, 0))
+    line = pl.BlockSpec((1, 128), lambda pair: (0, 0))
+    two = pl.BlockSpec((1, 2, 128), lambda pair: (pair, 0, 0))
+    low = lambda: jax.ShapeDtypeStruct((tokens, 256), jnp.bfloat16)
+    wide = pltpu.VMEM((tokens, 256), jnp.bfloat16)
+    both = pltpu.VMEM((2, tokens, 256), jnp.bfloat16)
+    return pl.pallas_call(
+        attend_back_kernel,
+        grid=(2,),
+        in_specs=[
+            column(0),
+            column(2),
+            column(0),
+            column(0),
+            column(0),
+            pl.BlockSpec((2, tokens, 128), lambda pair: (pair, 0, 0)),
+            whole,
+            column(0),
+            column(0),
+            whole,
+            whole,
+            line,
+            line,
+        ],
+        out_specs=[column(0), column(0), column(0), two, two],
+        out_shape=[
+            low(),
+            low(),
+            low(),
+            jax.ShapeDtypeStruct((2, 2, 128), jnp.float32),
+            jax.ShapeDtypeStruct((2, 2, 128), jnp.float32),
+        ],
+        scratch_shapes=[
+            wide,
+            wide,
+            pltpu.VMEM((128, tokens), jnp.bfloat16),
+            both,
+            both,
+            both,
+            pltpu.VMEM((128, tokens), jnp.float32),
+            pltpu.VMEM((tokens, 128), jnp.float32),
+            pltpu.VMEM((tokens, 128), jnp.float32),
+        ],
+        compiler_params=pltpu.CompilerParams(vmem_limit_bytes=48 << 20),
+        cost_estimate=pl.CostEstimate(
+            flops=40 * tokens * tokens * 256,
+            bytes_accessed=tokens * 256 * 40,
+            transcendentals=4 * tokens * tokens,
+        ),
+        name="attend_back",
+    )(
+        qkv,
+        qkv,
+        queries,
+        keys,
+        values,
+        extra,
+        hot,
+        grads,
+        attended,
+        cos_part,
+        sin_part,
+        q_gain,
+        k_gain,
+    )
+
+
+def local_split(
+    inputs,
+    variate_ids,
+    time_ids,
+    attn_gain,
+    query_weight,
+    key_weight,
+    value_weight,
+    out_weight,
+    query_gain,
+    key_gain,
+    variate_bias,
+    ffn_gain,
+    gate_weight,
+    up_weight,
+    down_weight,
+    out_grad,
+):
+    low = jnp.bfloat16
+    wide = jnp.float32
+    dp_at = lax.axis_index("dp")
+    seq_at = lax.axis_index("seq")
+    core = seq_at & 1
+    level = seq_at >> 1
+    batch = level >> 1
+    parity = level & 1
+    piece = inputs.shape[2]
+    tokens = 8 * piece
+    swap_core = lambda values: swap_seq(values, 1)
+    swap_level = lambda values, mask: swap_seq(values, 2 * mask)
+
+    def gather_sequence(pair):
+        mine = at_index(pair, batch)
+        other = at_index(pair, 1 - batch)
+        far = swap_level(other, 2)
+        near = swap_level(mine, 1)
+        last = swap_level(far, 1)
+        four = jnp.stack([mine, near, far, last])
+        return jnp.stack([four, swap_core(four)])
+
+    own_x = inputs[:, 0]
+    ids = gather_sequence(jnp.stack([variate_ids[:, 0], time_ids[:, 0]], axis=1))
+    sequence = gather_sequence(own_x).reshape(tokens, D)
+
+    gain_low = attn_gain.astype(low).astype(wide)
+    weights_low = jnp.stack([query_weight, key_weight, value_weight], axis=1).astype(low)
+    scaled = (weights_low.astype(wide) * gain_low[:, None, None]).astype(low)
+    scaled = scaled.reshape(32, 3, 2, 2, 256)
+    rows = ordered(
+        [at_index(scaled, core, 3), swap_core(at_index(scaled, 1 - core, 3))], core
+    ).reshape(64, 3, 2, 256)
+    same = at_index(rows, parity, 2).reshape(64, 768)
+    cross = at_index(rows, 1 - parity, 2).reshape(64, 768)
+    rows = ordered(
+        [same, swap_level(cross, 1), swap_level(same, 2), swap_level(cross, 3)], level
+    ).reshape(256, 768)
+    w_qkv = ordered([rows] + [swap_dp(rows, mask) for mask in (1, 2, 3)], dp_at).reshape(D, 768)
+
+    with_gain = jnp.concatenate(
+        [out_weight.astype(low), jnp.pad(ffn_gain.astype(low)[:, None], ((0, 0), (0, 127)))], axis=1
+    )
+    rows = ordered([with_gain] + [swap_level(with_gain, mask) for mask in (1, 2, 3)], level)
+    rows = ordered([rows] + [swap_dp(rows, mask) for mask in (1, 2, 3)], dp_at)
+    w_out = ordered([rows, swap_core(rows)], core)
+    w_out = jnp.transpose(w_out, (1, 2, 0, 3, 4)).reshape(D, D + 128)
+    gain_two = w_out[:, D].astype(wide)[None, :]
+    w_out = w_out[:, :D]
+
+    own_dy = out_grad[:, 0].reshape(2 * piece, D)
+    all_dy = jnp.concatenate([own_dy] + [swap_dp(own_dy, mask) for mask in (1, 2, 3)])
+
+    ffn_local = jnp.stack([gate_weight, up_weight, down_weight]).astype(low)
+    w_ffn = lax.all_gather(ffn_local, "seq", axis=1, tiled=True)
+
+    kinds = ids[:, :, 0].reshape(tokens, 1)
+    times = ids[:, :, 1].reshape(tokens, 1).astype(wide)
+    lane = lax.broadcasted_iota(jnp.int32, (1, 128), 1)
+    hot = jnp.where(
+        lane < LSE_LANE, (kinds == lane % 8).astype(wide), jnp.where(lane < LSE_LANE + 3, 1.0, 0.0)
+    ).astype(low)
+    half = HD // 2
+    frequency = 10000.0 ** (-(lane % half).astype(wide) / half)
+    angles = times * frequency
+    cos_part = jnp.cos(angles)
+    sin_part = jnp.sin(angles) * jnp.where(lane % HD < half, -1.0, 1.0)
+    q_gain = jnp.tile(query_gain, 2)[None, :]
+    k_gain = jnp.tile(key_gain, 2)[None, :]
+    group = 2 * parity + core
+    gaps = at_index((variate_bias[0] - variate_bias[1]).reshape(4, 4), group)
+    first, second, third = three_parts(gaps)
+    bias_rows = jnp.where(
+        lane < 8,
+        first[:, None],
+        jnp.where(
+            lane < 16, second[:, None], jnp.where(lane < LSE_LANE, third[:, None], 0.0)
+        ),
+    ).reshape(2, 2, 128)
+
+    seq_wide = sequence.astype(wide)
+    unit = (seq_wide * rms_scale(seq_wide)).astype(low)
+    qkv = product(unit, w_qkv)
+    attended, *saved = attend(qkv, cos_part, sin_part, hot, q_gain, k_gain, bias_rows)
+
+    parts = attended.reshape(2, 4, piece, 256)
+    both = jnp.stack([parts[0], swap_core(parts[1])], axis=2)
+    arrived = [both[0]] + [swap_level(both[mask], mask) for mask in (1, 2, 3)]
+    split = jnp.stack(arrived).reshape(2, 2, piece, 2, 256)
+    split = jnp.where(batch == 1, split[::-1], split)
+    split = jnp.where(parity == 1, split[:, ::-1], split)
+    split = jnp.where(core == 1, split[:, :, :, ::-1], split)
+    own_att = jnp.transpose(split, (0, 2, 1, 3, 4)).reshape(2 * piece, D)
+
+    own_wide = own_x.reshape(2 * piece, D).astype(wide)
+    middle = own_wide + product(own_att, w_out)
+    inv_two = rms_scale(middle)
+    normed_two = (middle * inv_two * gain_two).astype(low)
+    all_two = jnp.concatenate([normed_two] + [swap_dp(normed_two, mask) for mask in (1, 2, 3)])
+
+    w_gate, w_up, w_down = w_ffn[0], w_ffn[1], w_ffn[2]
+    gate_pre = times_transposed(all_two, w_gate)
+    up_pre = times_transposed(all_two, w_up)
+    grad_hidden = times_transposed(all_dy, w_down)
+    gate_sig = jax.nn.sigmoid(gate_pre)
+    hidden = (gate_pre * gate_sig * up_pre).astype(low)
+    grad_gate = (grad_hidden * up_pre * gate_sig * (1.0 + gate_pre * (1.0 - gate_sig))).astype(low)
+    grad_up = (grad_hidden * gate_pre * gate_sig).astype(low)
+
+    def scatter_tokens(partial):
+        chunks = partial.reshape(4, 2 * piece, D)
+        total = chunks[0]
+        for mask in (1, 2, 3):
+            total = total + swap_dp(chunks[mask].astype(low), mask).astype(wide)
+        return total
+
+    grad_two = scatter_tokens(product(grad_gate, w_gate) + product(grad_up, w_up))
+    result = middle + scatter_tokens(product(hidden, w_down))
+    ffn_grads = jnp.stack(
+        [
+            rows_inner(grad_gate, all_two).astype(low),
+            rows_inner(grad_up, all_two).astype(low),
+            rows_inner(hidden, all_dy).astype(low),
+        ]
+    )
+    ffn_grads = lax.psum_scatter(ffn_grads, "seq", scatter_dimension=1, tiled=True).astype(wide)
+
+    dy_wide = own_dy.astype(wide)
+    gain_two_part = jnp.sum(grad_two * middle * inv_two, axis=0)
+    grad_middle = dy_wide + norm_back(middle, inv_two, gain_two, grad_two)
+    middle_low = grad_middle.astype(low)
+    grad_att = times_transposed(middle_low, w_out).astype(low)
+    out_part = rows_inner(own_att, middle_low)
+
+    split = jnp.transpose(grad_att.reshape(2, piece, 2, 2, 256), (0, 2, 1, 3, 4))
+    split = jnp.where(batch == 1, split[::-1], split)
+    split = jnp.where(parity == 1, split[:, ::-1], split)
+    split = jnp.where(core == 1, split[:, :, :, ::-1], split)
+    split = split.reshape(4, piece, 2, 256)
+    arrived = jnp.stack([split[0]] + [swap_level(split[mask], mask) for mask in (1, 2, 3)])
+    grads = jnp.stack([arrived[:, :, 0], swap_core(arrived[:, :, 1])]).reshape(tokens, 256)
+
+    dq, dk, dv, gain_sums, bias_sums = attend_back(
+        qkv, saved, hot, grads, attended, cos_part, sin_part, q_gain, k_gain
+    )
+    dqkv = jnp.concatenate([dq, dk, dv], axis=1)
+
+    qkv_part = rows_inner(unit, dqkv).astype(low).reshape(4, 4, 2, 32, 768)
+    other = swap_core(at_index(qkv_part, 1 - core, 2))
+    qkv_part = jnp.stack([at_index(qkv_part, core, 2), other], axis=2)
+    total = at_index(qkv_part, dp_at).astype(wide)
+    for mask in (1, 2, 3):
+        total = total + swap_dp(at_index(qkv_part, dp_at ^ mask), mask).astype(wide)
+    total = total.astype(low)
+    same = at_index(total, level).astype(wide) + swap_level(at_index(total, level ^ 2), 2).astype(
+        wide
+    )
+    cross = swap_level(at_index(total, level ^ 1), 1).astype(wide) + swap_level(
+        at_index(total, level ^ 3), 3
+    ).astype(wide)
+    split = jnp.stack([same, cross]).reshape(2, 2, 32, 3, 256)
+    split = jnp.where(parity == 1, split[::-1], split)
+    split = jnp.where(core == 1, split[:, ::-1], split)
+    unit_grads = jnp.transpose(split, (3, 2, 0, 1, 4)).reshape(3, 32, D)
+    gain_grad = jnp.sum(unit_grads * jnp.transpose(weights_low, (1, 0, 2)).astype(wide), axis=(0, 2))
+    qkv_grads = unit_grads * gain_low[None, :, None]
+
+    unit_back = times_transposed(dqkv, w_qkv).reshape(2, 4, piece, D)
+    total = unit_back[0] + swap_core(unit_back[1].astype(low)).astype(wide)
+    passed = total[2] + swap_level(total[3].astype(low), 1).astype(wide)
+    kept = total[0] + swap_level(total[1].astype(low), 1).astype(wide)
+    passed = swap_level(passed.astype(low), 2).astype(wide)
+    back = jnp.stack([kept, passed])
+    back = jnp.where(batch == 1, back[::-1], back).reshape(2 * piece, D)
+    inv_one = rms_scale(own_wide)
+    inner = jnp.mean(back * own_wide, axis=-1, keepdims=True)
+    input_grad = grad_middle + inv_one * back - own_wide * (inv_one * inv_one * inv_one) * inner
+
+    out_part = out_part.reshape(4, 4, 2, 32, D)
+    total = at_index(out_part, core, 2) + swap_core(
+        at_index(out_part, 1 - core, 2).astype(low)
+    ).astype(wide)
+    kept = at_index(total, dp_at)
+    for mask in (1, 2, 3):
+        kept = kept + swap_dp(at_index(total, dp_at ^ mask).astype(low), mask).astype(wide)
+    out_grads = at_index(kept, level)
+    for mask in (1, 2, 3):
+        out_grads = out_grads + swap_level(
+            at_index(kept, level ^ mask).astype(low), mask
+        ).astype(wide)
+
+    gain_sums = jnp.sum(gain_sums, axis=0).reshape(2, 2, HD)
+    gain_sums = jnp.sum(gain_sums, axis=1).reshape(128)
+    bias_sums = bias_sums.reshape(4, 128)
+    same = jnp.sum(bias_sums[:, :8], axis=1)
+    pair = jnp.stack([same, bias_sums[:, LSE_LANE] - same])
+    placed = jnp.where(jnp.arange(4)[None, :, None] == group, pair[:, None, :], 0.0).reshape(2 * H)
+    small = jnp.concatenate([gain_two_part, gain_sums, placed, jnp.zeros((96,), wide)])
+    small = small.reshape(10, 128)
+    for swap, masks in ((swap_dp, (1, 2, 3)), (swap_level, (1, 2, 3)), (swap_seq, (1,))):
+        moved = [small] + [swap(small, mask) for mask in masks]
+        while len(moved) > 1:
+            moved = [left + right for left, right in zip(moved[::2], moved[1::2])]
+        small = moved[0]
+    small = small.reshape(1280)
+    gain_two_grad = lax.dynamic_slice_in_dim(small, (dp_at * 8 + seq_at) * 32, 32)
+
+    shape = (2, 1, piece, D)
+    return (
+        result.astype(low).reshape(shape),
+        input_grad.astype(low).reshape(shape),
+        gain_grad,
+        qkv_grads[0],
+        qkv_grads[1],
+        qkv_grads[2],
+        out_grads,
+        small[D : D + HD],
+        small[D + HD : D + 2 * HD],
+        small[D + 2 * HD : D + 2 * HD + 2 * H].reshape(2, H),
+        gain_two_grad,
+        ffn_grads[0],
+        ffn_grads[1],
+        ffn_grads[2],
+    )
+
+
 def solution(mesh):
     placed = (
         P(None, "dp", "seq", None),
@@ -426,8 +1025,9 @@
         P(("dp", "seq"), None),
         P(None, "dp", "seq", None),
     )
+    split = mesh.shape["dp"] == 4 and mesh.shape["seq"] == 8
     return jax.shard_map(
-        local,
+        local_split if split else local,
         mesh=mesh,
         in_specs=placed,
         out_specs=(

time: 2020 us -> 453 us (0.22)
  waiting for transfers between devices: 1470 us -> 181 us
  matrix products: 209 us -> 47.2 us
  local copies, waits for them, and re-layouts: 146 us -> 40.1 us
  blocking collectives: 99.8 us -> 0 us
  starting transfers between devices: 1.55 us -> 72.3 us
  Pallas kernels: 0 us -> 33.3 us
    reduce_scatter x7 -> x1, waiting for transfers between devices: 1030 us -> 0.01 us  [local_split(): lax.psum_scatter(ffn_grads, 'seq', scatter_dimension=1, tiled=True)]
    all_gather x11 -> x1, waiting for transfers between devices: 412 us -> 0.01 us  [local_split(): w_ffn = lax.all_gather(ffn_local, 'seq', axis=1, tiled=True)]
    ppermute x0 -> x67, waiting for transfers between devices: none -> 181 us  [the longest x40 91.2 us: swap_seq(): return lax.ppermute(values, 'seq', [(at, at ^ mask) for at in range(8)])]
    unnamed x2 -> x0, blocking collectives: 80.5 us -> none
    ppermute x0 -> x67, starting transfers between devices: none -> 72.2 us  [the longest x40 38.8 us: swap_seq(): return lax.ppermute(values, 'seq', [(at, at ^ mask) for at in range(8)])]
    dot_general x28 -> x0, matrix products: 70.4 us -> none  [the longest x8 16.6 us: score_block(): jnp.einsum('sqhe,skhe->shqk', queries, key_rows, preferred_element_type=j...]
    unnamed x254 -> x119, local copies, waits for them, and re-layouts: 71.4 us -> 8.1 us
    dot_general x14 -> x5, matrix products: 47.3 us -> 13.7 us  [rows_inner(): lax.dot_general(left_side, right_side, (((0,), (0,)), ((), ())), preferre...]
  transfers between devices with their start and end apart: 22 -> 69, of which waited for: 18 -> 29; matrix products, arithmetic and copies ran while one was open for 15% -> 26% of each run, Pallas kernels for 0% -> 7%
where the time goes in v1:
time: 453 us; the launch traced here: 444 us
  waiting for transfers between devices  181 us (40%)
  starting transfers between devices  72.3 us (16%)
  other arithmetic  54.3 us (12%)
  matrix products  47.2 us (10%)
  local copies, waits for them, and re-layouts  40.1 us (9%)
  Pallas kernels  33.3 us (7%)
  between operations  15.9 us (4%)
    ppermute x40, waiting for transfers between devices, swap_seq(): return lax.ppermute(values, 'seq', [(at, at ^ mask) for at in range(8)])  91.2 us
    ppermute x27, waiting for transfers between devices, swap_dp(): return lax.ppermute(values, 'dp', [(at, at ^ mask) for at in range(4)])  90 us
    ppermute x40, starting transfers between devices, swap_seq(): return lax.ppermute(values, 'seq', [(at, at ^ mask) for at in range(8)])  38.8 us
    ppermute x27, starting transfers between devices, swap_dp(): return lax.ppermute(values, 'dp', [(at, at ^ mask) for at in range(4)])  33.4 us
    pallas_call x1, Pallas kernels, attend_back(): pl.pallas_call(attend_back_kernel, grid=(2,), in_specs=[column(0), column...  22 us
    dot_general x5, matrix products, times_transposed(): lax.dot_general(left_side, right_side, (((1,), (1,)), ((), ())), preferre...  18.1 us
    dot_general x5, matrix products, product(): return jnp.dot(left_side, right_side, preferred_element_type=jnp.float32)  15.4 us
    dot_general x5, matrix products, rows_inner(): lax.dot_general(left_side, right_side, (((0,), (0,)), ((), ())), preferre...  13.7 us
  transfers between devices with their start and end apart: 69, of which 29 were waited for; matrix products, arithmetic and copies ran while one was open for 26% of the time, Pallas kernels for 7%

profile of v1, /device:TPU:0, one launch (start us, length us, event | category | flops | bytes accessed | tf_op | source)
XLA Modules:
  0.0 444.4 jit_solution(6812670939620479636)
XLA Ops:
  41.0 26.6 %collective-permute-done.5 = bf16[64,768]{1,0:T(8,128)(2,1)S(1)} collective-permute-done((bf16[64,768]{1,0:T(8,128)(2,1)S(1)}, bf16[64,768]{1,0:T(8,128)(2,1)S(1)}, u32[]{:S(2)}, u32[]{:S(2)}) %collective-permute-start.5) | collective-permute-done | bytes 98336 | tf_op jit(solution)/shard_map/ppermute | solution.py:413
  69.1 3.7 collective-permute-done.6
  79.0 19.7 %collective-permute-done.23 = bf16[4,32,1152]{2,1,0:T(8,128)(2,1)S(1)} collective-permute-done((bf16[4,32,1152]{2,1,0:T(8,128)(2,1)S(1)}, bf16[4,32,1152]{2,1,0:T(8,128)(2,1)S(1)}, u32[]{:S(2)}, u32[]{:S(2)}) %collective-permute-start.23) | collective-permute-done | bytes 294944 | tf_op jit(solution)/shard_map/ppermute | solution.py:417
  102.3 4.3 collective-permute-done.2
  107.8 9.4 %collective-permute-done.9 = bf16[256,768]{1,0:T(8,128)(2,1)S(1)} collective-permute-done((bf16[256,768]{1,0:T(8,128)(2,1)S(1)}, bf16[256,768]{1,0:T(8,128)(2,1)S(1)}, u32[]{:S(2)}, u32[]{:S(2)}) %collective-permute-start.9) | collective-permute-done | bytes 393248 | tf_op jit(solution)/shard_map/ppermute | solution.py:417
  120.5 11.3 %attend.1 = (bf16[1024,256]{1,0:T(8,128)(2,1)S(1)}, bf16[1024,256]{1,0:T(8,128)(2,1)S(1)}, bf16[1024,256]{1,0:T(8,128)(2,1)S(1)}, bf16[1024,256]{1,0:T(8,128)(2,1)S(1)}, bf16[4,1024,128]{2,1,0:T(8,128)(2,1)S(1)}) custom-call(f32[1024,768]{1,0:T(8,128)S(1)} %fusion.95.q_in.k_in.v_in, f32[1024,768]{1,0:T(8,128)S(1)} %fusion.95.q_in.k_in.v_in, ...), custom_call_target="tpu_custom_call" | custom-call | flops 4294967296 | bytes 7864320 | tf_op jit(solution)/shard_map/attend/pallas_call | solution.py:652
  133.7 4.0 collective-permute-start.18
  138.8 3.4 collective-permute-done.18
  142.2 5.7 %collective-permute-done.17 = bf16[128,2,256]{2,0,1:T(8,128)(2,1)S(1)} collective-permute-done((bf16[128,2,256]{2,0,1:T(8,128)(2,1)S(1)}, bf16[128,2,256]{2,0,1:T(8,128)(2,1)S(1)}, u32[]{:S(2)}, u32[]{:S(2)}) %collective-permute-start.17) | collective-permute-done | bytes 131104 | tf_op jit(solution)/shard_map/ppermute | solution.py:413
  151.1 6.0 %rev.29 = bf16[2,2,128,2,256]{4,3,1,2,0:T(2,128)(2,1)} reverse(bf16[2,2,128,2,256]{4,3,1,2,0:T(2,128)(2,1)} %broadcast_select_fusion.3), dimensions={3} | reverse | bytes 1048576 | tf_op jit(solution)/shard_map/rev | solution.py:874
  172.9 8.8 %collective-permute-done.28 = bf16[256,1024]{1,0:T(8,128)(2,1)S(1)} collective-permute-done((bf16[256,1024]{1,0:T(8,128)(2,1)S(1)}, bf16[256,1024]{1,0:T(8,128)(2,1)S(1)}, u32[]{:S(2)}, u32[]{:S(2)}) %collective-permute-start.28) | collective-permute-done | bytes 524320 | tf_op jit(solution)/shard_map/ppermute | solution.py:417
  183.2 8.7 %collective-permute-done.27 = bf16[256,1024]{1,0:T(8,128)(2,1)S(1)} collective-permute-done((bf16[256,1024]{1,0:T(8,128)(2,1)S(1)}, bf16[256,1024]{1,0:T(8,128)(2,1)S(1)}, u32[]{:S(2)}, u32[]{:S(2)}) %collective-permute-start.27) | collective-permute-done | bytes 524320 | tf_op jit(solution)/shard_map/ppermute | solution.py:417
  192.7 4.6 %fusion.2 = f32[1024,1024]{1,0:T(8,128)S(1)} fusion(bf16[3,1024,1024]{2,1,0:T(8,128)(2,1)} %all-gather.2.cloned.1.call-done, bf16[256,1024]{1,0:T(8,128)(2,1)} %copy-done.47, bf16[256,1024]{1,0:T(8,128)(2,1)} %copy-done.49, bf16[256,1024]{1,0:T(8,128)(2,1)} %collective-permute-done.26, bf16[256,1024]{1,0:T(8,128)(2,1)S(1)} %multiply_convert_fusion.4), kind=kOutput, calls=%fused_computation.33 | convolution fusion | flops 2155872256 | bytes 8388608 | tf_op jit(solution)/shard_map/dot_general | solution.py:68
  197.3 3.4 fusion.3
  203.1 6.1 %multiply_convert_fusion = (bf16[1024,1024]{1,0:T(8,128)(2,1)S(1)}, bf16[1024,1024]{1,0:T(8,128)(2,1)S(1)}, bf16[1024,1024]{1,0:T(8,128)(2,1)S(1)}) fusion(f32[1024,1024]{1,0:T(8,128)S(1)} %fusion.2, f32[1024,1024]{1,0:T(8,128)S(1)} %fusion.3, bf16[3,1024,1024]{2,1,0:T(8,128)(2,1)S(1)} %copy-done.46, bf16[256,1024]{1,0:T(8,128)(2,1)} %collective-permute-done.34, ...), kind=kOutput, calls=%fused_computation.3 | convolution fusion | flops 2172649472 | bytes 18874368 | tf_op jit(solution)/shard_map/dot_general | solution.py:68
  211.5 4.3 fusion.93
  220.5 4.4 fusion.94
  229.1 3.9 convert_bitcast_fusion
  233.0 3.5 convert_bitcast_fusion.1
  236.5 3.7 convert_bitcast_fusion.2
  247.6 7.9 %collective-permute-done.31 = bf16[256,1024]{1,0:T(8,128)(2,1)S(1)} collective-permute-done((bf16[256,1024]{1,0:T(8,128)(2,1)}, bf16[256,1024]{1,0:T(8,128)(2,1)S(1)}, u32[]{:S(2)}, u32[]{:S(2)}) %collective-permute-start.31) | collective-permute-done | bytes 524320 | tf_op jit(solution)/shard_map/ppermute | solution.py:417
  255.5 9.7 %collective-permute-done.30 = bf16[256,1024]{1,0:T(8,128)(2,1)} collective-permute-done((bf16[256,1024]{1,0:T(8,128)(2,1)}, bf16[256,1024]{1,0:T(8,128)(2,1)}, u32[]{:S(2)}, u32[]{:S(2)}) %collective-permute-start.30) | collective-permute-done | bytes 524320 | tf_op jit(solution)/shard_map/ppermute | solution.py:417
  273.4 5.7 %rev.32 = bf16[2,2,128,2,256]{4,3,1,2,0:T(2,128)(2,1)} reverse(bf16[2,2,128,2,256]{4,3,1,2,0:T(2,128)(2,1)} %broadcast_select_fusion.2), dimensions={3} | reverse | bytes 1048576 | tf_op jit(solution)/shard_map/rev | solution.py:920
  285.1 4.0 fusion
  292.1 12.2 %collective-permute-done.39 = bf16[128,2,256]{2,0,1:T(8,128)(2,1)} collective-permute-done((bf16[128,2,256]{2,0,1:T(8,128)(2,1)}, bf16[128,2,256]{2,0,1:T(8,128)(2,1)}, u32[]{:S(2)}, u32[]{:S(2)}) %collective-permute-start.39) | collective-permute-done | bytes 131104 | tf_op jit(solution)/shard_map/ppermute | solution.py:413
  308.9 22.0 %attend_back.1 = (bf16[1024,256]{1,0:T(8,128)(2,1)S(1)}, bf16[1024,256]{1,0:T(8,128)(2,1)S(1)}, bf16[1024,256]{1,0:T(8,128)(2,1)S(1)}, f32[2,2,128]{2,1,0:T(2,128)S(1)}, f32[2,2,128]{2,1,0:T(2,128)S(1)}) custom-call(f32[1024,768]{1,0:T(8,128)} %copy-done, f32[1024,768]{1,0:T(8,128)} %copy-done, bf16[1024,256]{1,0:T(8,128)(2,1)S(1)} %copy-done.3, ...), custom_call_target="tpu_custom_call" | custom-call | flops 10737418240 | bytes 10485760 | tf_op jit(solution)/shard_map/attend_back/pallas_call | solution.py:704
  357.1 5.0 %collective-permute-done.56 = bf16[4,32,1024]{2,1,0:T(8,128)(2,1)} collective-permute-done((bf16[4,32,1024]{2,1,0:T(8,128)(2,1)}, bf16[4,32,1024]{2,1,0:T(8,128)(2,1)}, u32[]{:S(2)}, u32[]{:S(2)}) %collective-permute-start.56) | collective-permute-done | bytes 262176 | tf_op jit(solution)/shard_map/ppermute | solution.py:417
  362.1 5.2 %collective-permute-done.55 = bf16[4,32,1024]{2,1,0:T(8,128)(2,1)} collective-permute-done((bf16[4,32,1024]{2,1,0:T(8,128)(2,1)S(1)}, bf16[4,32,1024]{2,1,0:T(8,128)(2,1)}, u32[]{:S(2)}, u32[]{:S(2)}) %collective-permute-start.55) | collective-permute-done | bytes 262176 | tf_op jit(solution)/shard_map/ppermute | solution.py:417
  380.9 6.4 %collective-permute-done.49 = bf16[4,2,32,768]{3,2,1,0:T(8,128)(2,1)S(1)} collective-permute-done((bf16[4,2,32,768]{3,2,1,0:T(8,128)(2,1)S(1)}, bf16[4,2,32,768]{3,2,1,0:T(8,128)(2,1)S(1)}, u32[]{:S(2)}, u32[]{:S(2)}) %collective-permute-start.49) | collective-permute-done | bytes 393248 | tf_op jit(solution)/shard_map/ppermute | solution.py:417
  387.3 6.5 %collective-permute-done.48 = bf16[4,2,32,768]{3,2,1,0:T(8,128)(2,1)S(1)} collective-permute-done((bf16[4,2,32,768]{3,2,1,0:T(8,128)(2,1)S(1)}, bf16[4,2,32,768]{3,2,1,0:T(8,128)(2,1)S(1)}, u32[]{:S(2)}, u32[]{:S(2)}) %collective-permute-start.48) | collective-permute-done | bytes 393248 | tf_op jit(solution)/shard_map/ppermute | solution.py:417
  403.2 12.2 %collective-permute-done.52 = bf16[2,32,768]{2,1,0:T(8,128)(2,1)S(1)} collective-permute-done((bf16[2,32,768]{2,1,0:T(8,128)(2,1)S(1)}, bf16[2,32,768]{2,1,0:T(8,128)(2,1)S(1)}, u32[]{:S(2)}, u32[]{:S(2)}) %collective-permute-start.52) | collective-permute-done | bytes 98336 | tf_op jit(solution)/shard_map/ppermute | solution.py:413
  421.0 11.2 %collective-permute-done.45 = bf16[128,1024]{1,0:T(8,128)(2,1)S(1)} collective-permute-done((bf16[128,1024]{1,0:T(8,128)(2,1)S(1)}, bf16[128,1024]{1,0:T(8,128)(2,1)S(1)}, u32[]{:S(2)}, u32[]{:S(2)}) %collective-permute-start.45) | collective-permute-done | bytes 262176 | tf_op jit(solution)/shard_map/ppermute | solution.py:413
  (396 shorter events, 175.0 us)
Async XLA Ops:
  7.2 185.5 %all-gather.2.cloned.1.call-start = ((), (), s32[]{:S(2)}) async-start(), calls=%async_computation.1 | async-start | bytes 7077888 | tf_op jit(solution)/shard_map/all_gather | solution.py:837
  9.5 25.6 %collective-permute-start.19 = (bf16[32,1152]{1,0:T(8,128)(2,1)}, bf16[32,1152]{1,0:T(8,128)(2,1)S(1)}, u32[]{:S(2)}, u32[]{:S(2)}) collective-permute-start(bf16[32,1152]{1,0:T(8,128)(2,1)} %fusion.68), channel_id=1, source_target_pairs={{0,2},{1,3},{2,0},{3,1},{4,6},{5,7},{6,4},{7,5},{8,10},{9,11},{10,... | collective-permute-start | bytes 221192 | tf_op jit(solution)/shard_map/ppermute | solution.py:413
  12.6 22.7 %collective-permute-start.20 = (bf16[32,1152]{1,0:T(8,128)(2,1)}, bf16[32,1152]{1,0:T(8,128)(2,1)S(1)}, u32[]{:S(2)}, u32[]{:S(2)}) collective-permute-start(bf16[32,1152]{1,0:T(8,128)(2,1)} %fusion.68), channel_id=1, source_target_pairs={{0,4},{1,5},{2,6},{3,7},{4,0},{5,1},{6,2},{7,3},{8,12},{9,13},{10,... | collective-permute-start | bytes 221192 | tf_op jit(solution)/shard_map/ppermute | solution.py:413
  15.2 20.1 %collective-permute-start.21 = (bf16[32,1152]{1,0:T(8,128)(2,1)}, bf16[32,1152]{1,0:T(8,128)(2,1)S(1)}, u32[]{:S(2)}, u32[]{:S(2)}) collective-permute-start(bf16[32,1152]{1,0:T(8,128)(2,1)} %fusion.68), channel_id=1, source_target_pairs={{0,6},{1,7},{2,4},{3,5},{4,2},{5,3},{6,0},{7,1},{8,14},{9,15},{10,... | collective-permute-start | bytes 221192 | tf_op jit(solution)/shard_map/ppermute | solution.py:413
  23.8 410.8 %reduce-scatter.2.cloned.1.call-start = ((), (), s32[]{:S(2)}) async-start(), calls=%async_computation.2 | async-start | bytes 7077888 | tf_op jit(solution)/shard_map/reduce_scatter | solution.py:908
  28.4 47.5 %collective-permute-start.1 = (bf16[128,1024]{1,0:T(8,128)(2,1)}, bf16[128,1024]{1,0:T(8,128)(2,1)S(1)}, u32[]{:S(2)}, u32[]{:S(2)}) collective-permute-start(bf16[128,1024]{1,0:T(8,128)(2,1)} %get-tuple-element.152), channel_id=1, source_target_pairs={{0,4},{1,5},{2,6},{3,7},{4,0},{5,1},{6,2},{7,3},{8,12},{9,13},{10,... | collective-permute-start | bytes 786440 | tf_op jit(solution)/shard_map/ppermute | solution.py:413
  32.9 67.4 %collective-permute-start = (bf16[128,1024]{1,0:T(8,128)(2,1)}, bf16[128,1024]{1,0:T(8,128)(2,1)S(1)}, u32[]{:S(2)}, u32[]{:S(2)}) collective-permute-start(bf16[128,1024]{1,0:T(8,128)(2,1)} %get-tuple-element.151), channel_id=1, source_target_pairs={{0,2},{1,3},{2,0},{3,1},{4,6},{5,7},{6,4},{7,5},{8,10},{9,11},{10,... | collective-permute-start | bytes 786440 | tf_op jit(solution)/shard_map/ppermute | solution.py:413
  37.2 30.4 %collective-permute-start.5 = (bf16[64,768]{1,0:T(8,128)(2,1)S(1)}, bf16[64,768]{1,0:T(8,128)(2,1)S(1)}, u32[]{:S(2)}, u32[]{:S(2)}) collective-permute-start(bf16[64,768]{1,0:T(8,128)(2,1)S(1)} %bitcast.376), channel_id=1, source_target_pairs={{0,2},{1,3},{2,0},{3,1},{4,6},{5,7},{6,4},{7,5},{8,10},{9,11},{10,... | collective-permute-start | bytes 294920 | tf_op jit(solution)/shard_map/ppermute | solution.py:413
  39.1 35.2 %collective-permute-start.7 = (bf16[64,768]{1,0:T(8,128)(2,1)S(1)}, bf16[64,768]{1,0:T(8,128)(2,1)S(1)}, u32[]{:S(2)}, u32[]{:S(2)}) collective-permute-start(bf16[64,768]{1,0:T(8,128)(2,1)S(1)} %bitcast.377), channel_id=1, source_target_pairs={{0,6},{1,7},{2,4},{3,5},{4,2},{5,3},{6,0},{7,1},{8,14},{9,15},{10,... | collective-permute-start | bytes 294920 | tf_op jit(solution)/shard_map/ppermute | solution.py:413
  40.3 32.5 %collective-permute-start.6 = (bf16[64,768]{1,0:T(8,128)(2,1)S(1)}, bf16[64,768]{1,0:T(8,128)(2,1)S(1)}, u32[]{:S(2)}, u32[]{:S(2)}) collective-permute-start(bf16[64,768]{1,0:T(8,128)(2,1)S(1)} %bitcast.365), channel_id=1, source_target_pairs={{0,4},{1,5},{2,6},{3,7},{4,0},{5,1},{6,2},{7,3},{8,12},{9,13},{10,... | collective-permute-start | bytes 294920 | tf_op jit(solution)/shard_map/ppermute | solution.py:413
  72.8 25.9 %collective-permute-start.23 = (bf16[4,32,1152]{2,1,0:T(8,128)(2,1)S(1)}, bf16[4,32,1152]{2,1,0:T(8,128)(2,1)S(1)}, u32[]{:S(2)}, u32[]{:S(2)}) collective-permute-start(bf16[4,32,1152]{2,1,0:T(8,128)(2,1)S(1)} %pad_maximum_fusion.15), channel_id=1, source_target_pairs={{0,16},{8,24},{16,0},{24,8},{1,17},{9,25},{17,1},{25,9},{2,18},{10... | collective-permute-start | bytes 884744 | tf_op jit(solution)/shard_map/ppermute | solution.py:417
  74.3 25.9 %collective-permute-start.24 = (bf16[4,32,1152]{2,1,0:T(8,128)(2,1)S(1)}, bf16[4,32,1152]{2,1,0:T(8,128)(2,1)S(1)}, u32[]{:S(2)}, u32[]{:S(2)}) collective-permute-start(bf16[4,32,1152]{2,1,0:T(8,128)(2,1)S(1)} %pad_maximum_fusion.15), channel_id=1, source_target_pairs={{0,24},{8,16},{16,8},{24,0},{1,25},{9,17},{17,9},{25,1},{2,26},{10... | collective-permute-start | bytes 884744 | tf_op jit(solution)/shard_map/ppermute | solution.py:417
  75.9 124.9 %collective-permute-start.34 = (bf16[256,1024]{1,0:T(8,128)(2,1)}, bf16[256,1024]{1,0:T(8,128)(2,1)}, u32[]{:S(2)}, u32[]{:S(2)}) collective-permute-start(bf16[256,1024]{1,0:T(8,128)(2,1)} %bitcast.68), channel_id=1, source_target_pairs={{0,24},{8,16},{16,8},{24,0},{1,25},{9,17},{17,9},{25,1},{2,26},{10... | collective-permute-start | bytes 1572872 | tf_op jit(solution)/shard_map/ppermute | solution.py:417
  77.5 29.7 %collective-permute-start.8 = (bf16[256,768]{1,0:T(8,128)(2,1)S(1)}, bf16[256,768]{1,0:T(8,128)(2,1)S(1)}, u32[]{:S(2)}, u32[]{:S(2)}) collective-permute-start(bf16[256,768]{1,0:T(8,128)(2,1)S(1)} %bitcast.356), channel_id=1, source_target_pairs={{0,8},{8,0},{16,24},{24,16},{1,9},{9,1},{17,25},{25,17},{2,10},{10... | collective-permute-start | bytes 1179656 | tf_op jit(solution)/shard_map/ppermute | solution.py:417
  98.7 18.5 %collective-permute-start.9 = (bf16[256,768]{1,0:T(8,128)(2,1)S(1)}, bf16[256,768]{1,0:T(8,128)(2,1)S(1)}, u32[]{:S(2)}, u32[]{:S(2)}) collective-permute-start(bf16[256,768]{1,0:T(8,128)(2,1)S(1)} %bitcast.357), channel_id=1, source_target_pairs={{0,16},{8,24},{16,0},{24,8},{1,17},{9,25},{17,1},{25,9},{2,18},{10... | collective-permute-start | bytes 1179656 | tf_op jit(solution)/shard_map/ppermute | solution.py:417
  107.2 93.6 %collective-permute-start.33 = (bf16[256,1024]{1,0:T(8,128)(2,1)}, bf16[256,1024]{1,0:T(8,128)(2,1)}, u32[]{:S(2)}, u32[]{:S(2)}) collective-permute-start(bf16[256,1024]{1,0:T(8,128)(2,1)} %bitcast.68), channel_id=1, source_target_pairs={{0,16},{8,24},{16,0},{24,8},{1,17},{9,25},{17,1},{25,9},{2,18},{10... | collective-permute-start | bytes 1572872 | tf_op jit(solution)/shard_map/ppermute | solution.py:417
  167.8 24.0 %collective-permute-start.27 = (bf16[256,1024]{1,0:T(8,128)(2,1)S(1)}, bf16[256,1024]{1,0:T(8,128)(2,1)S(1)}, u32[]{:S(2)}, u32[]{:S(2)}) collective-permute-start(bf16[256,1024]{1,0:T(8,128)(2,1)S(1)} %multiply_convert_fusion.4), channel_id=1, source_target_pairs={{0,16},{8,24},{16,0},{24,8},{1,17},{9,25},{17,1},{25,9},{2,18},{10... | collective-permute-start | bytes 1572872 | tf_op jit(solution)/shard_map/ppermute | solution.py:417
  168.9 23.8 %collective-permute-start.26 = (bf16[256,1024]{1,0:T(8,128)(2,1)S(1)}, bf16[256,1024]{1,0:T(8,128)(2,1)}, u32[]{:S(2)}, u32[]{:S(2)}) collective-permute-start(bf16[256,1024]{1,0:T(8,128)(2,1)S(1)} %multiply_convert_fusion.4), channel_id=1, source_target_pairs={{0,8},{8,0},{16,24},{24,16},{1,9},{9,1},{17,25},{25,17},{2,10},{10... | collective-permute-start | bytes 1572872 | tf_op jit(solution)/shard_map/ppermute | solution.py:417
  181.7 21.4 %collective-permute-start.32 = (bf16[256,1024]{1,0:T(8,128)(2,1)}, bf16[256,1024]{1,0:T(8,128)(2,1)}, u32[]{:S(2)}, u32[]{:S(2)}) collective-permute-start(bf16[256,1024]{1,0:T(8,128)(2,1)} %bitcast.68), channel_id=1, source_target_pairs={{0,8},{8,0},{16,24},{24,16},{1,9},{9,1},{17,25},{25,17},{2,10},{10... | collective-permute-start | bytes 1572872 | tf_op jit(solution)/shard_map/ppermute | solution.py:417
  217.0 26.5 %collective-permute-start.37 = (bf16[256,1024]{1,0:T(8,128)(2,1)}, bf16[256,1024]{1,0:T(8,128)(2,1)}, u32[]{:S(2)}, u32[]{:S(2)}) collective-permute-start(bf16[256,1024]{1,0:T(8,128)(2,1)} %get-tuple-element.108), channel_id=1, source_target_pairs={{0,24},{8,16},{16,8},{24,0},{1,25},{9,17},{17,9},{25,1},{2,26},{10... | collective-permute-start | bytes 1572872 | tf_op jit(solution)/shard_map/ppermute | solution.py:417
  218.7 25.7 %collective-permute-start.36 = (bf16[256,1024]{1,0:T(8,128)(2,1)}, bf16[256,1024]{1,0:T(8,128)(2,1)}, u32[]{:S(2)}, u32[]{:S(2)}) collective-permute-start(bf16[256,1024]{1,0:T(8,128)(2,1)} %get-tuple-element.109), channel_id=1, source_target_pairs={{0,16},{8,24},{16,0},{24,8},{1,17},{9,25},{17,1},{25,9},{2,18},{10... | collective-permute-start | bytes 1572872 | tf_op jit(solution)/shard_map/ppermute | solution.py:417
  220.0 24.5 %collective-permute-start.35 = (bf16[256,1024]{1,0:T(8,128)(2,1)}, bf16[256,1024]{1,0:T(8,128)(2,1)}, u32[]{:S(2)}, u32[]{:S(2)}) collective-permute-start(bf16[256,1024]{1,0:T(8,128)(2,1)} %get-tuple-element.107), channel_id=1, source_target_pairs={{0,8},{8,0},{16,24},{24,16},{1,9},{9,1},{17,25},{25,17},{2,10},{10... | collective-permute-start | bytes 1572872 | tf_op jit(solution)/shard_map/ppermute | solution.py:417
  226.1 29.4 %collective-permute-start.31 = (bf16[256,1024]{1,0:T(8,128)(2,1)}, bf16[256,1024]{1,0:T(8,128)(2,1)S(1)}, u32[]{:S(2)}, u32[]{:S(2)}) collective-permute-start(bf16[256,1024]{1,0:T(8,128)(2,1)} %get-tuple-element.111), channel_id=1, source_target_pairs={{0,24},{8,16},{16,8},{24,0},{1,25},{9,17},{17,9},{25,1},{2,26},{10... | collective-permute-start | bytes 1572872 | tf_op jit(solution)/shard_map/ppermute | solution.py:417
  227.8 37.4 %collective-permute-start.30 = (bf16[256,1024]{1,0:T(8,128)(2,1)}, bf16[256,1024]{1,0:T(8,128)(2,1)}, u32[]{:S(2)}, u32[]{:S(2)}) collective-permute-start(bf16[256,1024]{1,0:T(8,128)(2,1)} %get-tuple-element.112), channel_id=1, source_target_pairs={{0,16},{8,24},{16,0},{24,8},{1,17},{9,25},{17,1},{25,9},{2,18},{10... | collective-permute-start | bytes 1572872 | tf_op jit(solution)/shard_map/ppermute | solution.py:417
  243.5 21.7 %collective-permute-start.29 = (bf16[256,1024]{1,0:T(8,128)(2,1)}, bf16[256,1024]{1,0:T(8,128)(2,1)S(1)}, u32[]{:S(2)}, u32[]{:S(2)}) collective-permute-start(bf16[256,1024]{1,0:T(8,128)(2,1)} %get-tuple-element.110), channel_id=1, source_target_pairs={{0,8},{8,0},{16,24},{24,16},{1,9},{9,1},{17,25},{25,17},{2,10},{10... | collective-permute-start | bytes 1572872 | tf_op jit(solution)/shard_map/ppermute | solution.py:417
  282.1 22.2 %collective-permute-start.39 = (bf16[128,2,256]{2,0,1:T(8,128)(2,1)}, bf16[128,2,256]{2,0,1:T(8,128)(2,1)}, u32[]{:S(2)}, u32[]{:S(2)}) collective-permute-start(bf16[128,2,256]{2,0,1:T(8,128)(2,1)} %get-tuple-element.142), channel_id=1, source_target_pairs={{0,4},{1,5},{2,6},{3,7},{4,0},{5,1},{6,2},{7,3},{8,12},{9,13},{10,... | collective-permute-start | bytes 393224 | tf_op jit(solution)/shard_map/ppermute | solution.py:413
  282.6 21.7 %collective-permute-start.38 = (bf16[128,2,256]{2,0,1:T(8,128)(2,1)}, bf16[128,2,256]{2,0,1:T(8,128)(2,1)}, u32[]{:S(2)}, u32[]{:S(2)}) collective-permute-start(bf16[128,2,256]{2,0,1:T(8,128)(2,1)} %get-tuple-element.143), channel_id=1, source_target_pairs={{0,2},{1,3},{2,0},{3,1},{4,6},{5,7},{6,4},{7,5},{8,10},{9,11},{10,... | collective-permute-start | bytes 393224 | tf_op jit(solution)/shard_map/ppermute | solution.py:413
  307.6 41.7 %collective-permute-start.53 = (bf16[4,4,32,1024]{3,2,1,0:T(8,128)(2,1)}, bf16[4,4,32,1024]{3,2,1,0:T(8,128)(2,1)}, u32[]{:S(2)}, u32[]{:S(2)}) collective-permute-start(bf16[4,4,32,1024]{3,2,1,0:T(8,128)(2,1)} %fusion.16), channel_id=1, source_target_pairs={{0,1},{1,0},{2,3},{3,2},{4,5},{5,4},{6,7},{7,6},{8,9},{9,8},{10,11... | collective-permute-start | bytes 3145736 | tf_op jit(solution)/shard_map/ppermute | solution.py:413
  341.0 38.3 %collective-permute-start.42 = (bf16[4,128,1024]{2,1,0:T(8,128)(2,1)}, bf16[4,128,1024]{2,1,0:T(8,128)(2,1)}, u32[]{:S(2)}, u32[]{:S(2)}) collective-permute-start(bf16[4,128,1024]{2,1,0:T(8,128)(2,1)} %bitcast.86), channel_id=1, source_target_pairs={{0,1},{1,0},{2,3},{3,2},{4,5},{5,4},{6,7},{7,6},{8,9},{9,8},{10,11... | collective-permute-start | bytes 3145736 | tf_op jit(solution)/shard_map/ppermute | solution.py:413
  348.2 24.8 %collective-permute-start.46 = (bf16[4,4,32,768]{3,2,1,0:T(8,128)(2,1)}, bf16[4,4,32,768]{3,2,1,0:T(8,128)(2,1)}, u32[]{:S(2)}, u32[]{:S(2)}) collective-permute-start(bf16[4,4,32,768]{3,2,1,0:T(8,128)(2,1)} %get-tuple-element.119), channel_id=1, source_target_pairs={{0,1},{1,0},{2,3},{3,2},{4,5},{5,4},{6,7},{7,6},{8,9},{9,8},{10,11... | collective-permute-start | bytes 2359304 | tf_op jit(solution)/shard_map/ppermute | solution.py:413
  396.7 22.1 %collective-permute-start.43 = (bf16[128,1024]{1,0:T(8,128)(2,1)}, bf16[128,1024]{1,0:T(8,128)(2,1)S(1)}, u32[]{:S(2)}, u32[]{:S(2)}) collective-permute-start(bf16[128,1024]{1,0:T(8,128)(2,1)} %get-tuple-element.129), channel_id=1, source_target_pairs={{0,2},{1,3},{2,0},{3,1},{4,6},{5,7},{6,4},{7,5},{8,10},{9,11},{10,... | collective-permute-start | bytes 786440 | tf_op jit(solution)/shard_map/ppermute | solution.py:413
  398.4 20.3 %collective-permute-start.44 = (bf16[128,1024]{1,0:T(8,128)(2,1)}, bf16[128,1024]{1,0:T(8,128)(2,1)S(1)}, u32[]{:S(2)}, u32[]{:S(2)}) collective-permute-start(bf16[128,1024]{1,0:T(8,128)(2,1)} %get-tuple-element.130), channel_id=1, source_target_pairs={{0,2},{1,3},{2,0},{3,1},{4,6},{5,7},{6,4},{7,5},{8,10},{9,11},{10,... | collective-permute-start | bytes 786440 | tf_op jit(solution)/shard_map/ppermute | solution.py:413
  (94 other events, 718.7 us)
Sparse Core Ops, SparseCore 0:
  23.9 78.8 all-gather.1
  243.6 76.1 reduce-scatter.1

commit v2 on v1

--- a/solution.py
+++ b/solution.py
@@ -1,3 +1,4 @@
+import functools
 import math
 
 import jax
@@ -428,6 +429,10 @@
     return jnp.stack([pick(pieces, own ^ at) for at in range(len(pieces))])
 
 
+def together(*values):
+    return lax.optimization_barrier(values)
+
+
 def at_index(values, index, axis=0):
     return lax.dynamic_index_in_dim(values, index, axis, keepdims=False)
 
@@ -467,6 +472,7 @@
     return first, second, third
 
 
+GRANT = 60 << 20
 BQ = 256
 BK = 256
 LSE_LANE = 24
@@ -482,7 +488,8 @@
     q_gain,
     k_gain,
     bias_in,
-    att_out,
+    near_out,
+    far_out,
     qs_out,
     ks_out,
     vs_out,
@@ -530,7 +537,17 @@
             extra = jnp.where(lane == LSE_LANE + 1, second, extra)
             extra = jnp.where(lane == LSE_LANE + 2, third, extra)
             ext_out[head, rows, :] = extra.astype(jnp.bfloat16)
-        att_out[rows, :] = jnp.where(lane < HD, results[0], results[1]).astype(jnp.bfloat16)
+        result = jnp.where(lane < HD, results[0], results[1]).astype(jnp.bfloat16)
+        half = near_out.shape[0]
+
+        @pl.when(block < half // BQ)
+        def _():
+            near_out[pl.ds(pl.multiple_of(block * BQ, BQ), BQ), :] = result
+
+        @pl.when(block >= half // BQ)
+        def _():
+            far_out[pl.ds(pl.multiple_of(block * BQ - half, BQ), BQ), :] = result
+
         return carry
 
     lax.fori_loop(0, q_in.shape[0] // BQ, step, 0)
@@ -544,15 +561,15 @@
     vs_in,
     ext_in,
     hot_in,
-    grad_in,
-    att_in,
+    grad_near,
+    grad_far,
+    att_near,
+    att_far,
     cos_in,
     sin_in,
     q_gain,
     k_gain,
-    dq_out,
-    dk_out,
-    dv_out,
+    out,
     gain_out,
     bias_out,
     kx,
@@ -573,8 +590,9 @@
     kt[...] = keys.astype(jnp.float32).T.astype(jnp.bfloat16)
     vx[:, :128] = vs_in[...]
     vx[:, 128:] = jnp.where(lane % HD < 3, 1.0, 0.0).astype(jnp.bfloat16)
-    grads = grad_in[...].astype(jnp.float32)
-    delta = exact(grads * att_in[...].astype(jnp.float32), head_block(1.0))
+    grads = jnp.concatenate([grad_near[...], grad_far[...]]).astype(jnp.float32)
+    results = jnp.concatenate([att_near[...], att_far[...]]).astype(jnp.float32)
+    delta = exact(grads * results, head_block(1.0))
     first, second, third = three_parts(-delta)
     parts = jnp.where(
         lane % HD == 0,
@@ -636,9 +654,9 @@
 
     dq, dq_gain = finish(q_in[...], dqt[...].T * HD**-0.5, q_gain[...])
     dk, dk_gain = finish(k_in[...], dk_sum[...], k_gain[...])
-    dq_out[...] = dq.astype(jnp.bfloat16)
-    dk_out[...] = dk.astype(jnp.bfloat16)
-    dv_out[...] = dv_sum[...].astype(jnp.bfloat16)
+    out[0] = dq.astype(jnp.bfloat16)
+    out[1] = dk.astype(jnp.bfloat16)
+    out[2] = dv_sum[...].astype(jnp.bfloat16)
     gain_out[0, 0:1, :] = dq_gain
     gain_out[0, 1:2, :] = dk_gain
 
@@ -646,6 +664,7 @@
 def attend(qkv, cos_part, sin_part, hot, q_gain, k_gain, bias_rows):
     tokens = qkv.shape[0]
     column = lambda shift: pl.BlockSpec((tokens, 128), lambda pair: (0, pair + shift))
+    half = pl.BlockSpec((tokens // 2, 128), lambda pair: (0, pair))
     whole = pl.BlockSpec((tokens, 128), lambda pair: (0, 0))
     line = pl.BlockSpec((1, 128), lambda pair: (0, 0))
     low = lambda: jax.ShapeDtypeStruct((tokens, 256), jnp.bfloat16)
@@ -664,14 +683,16 @@
             pl.BlockSpec((1, 2, 128), lambda pair: (pair, 0, 0)),
         ],
         out_specs=[
-            column(0),
+            half,
+            half,
             column(0),
             column(0),
             column(0),
             pl.BlockSpec((2, tokens, 128), lambda pair: (pair, 0, 0)),
         ],
         out_shape=[
-            low(),
+            jax.ShapeDtypeStruct((tokens // 2, 256), jnp.bfloat16),
+            jax.ShapeDtypeStruct((tokens // 2, 256), jnp.bfloat16),
             low(),
             low(),
             low(),
@@ -681,7 +702,7 @@
             pltpu.VMEM((tokens, 256), jnp.bfloat16),
             pltpu.VMEM((tokens, 256), jnp.bfloat16),
         ],
-        compiler_params=pltpu.CompilerParams(vmem_limit_bytes=40 << 20),
+        compiler_params=pltpu.CompilerParams(vmem_limit_bytes=GRANT),
         cost_estimate=pl.CostEstimate(
             flops=16 * tokens * tokens * 256,
             bytes_accessed=tokens * 256 * 30,
@@ -695,10 +716,10 @@
     queries, keys, values, extra = saved
     tokens = qkv.shape[0]
     column = lambda shift: pl.BlockSpec((tokens, 128), lambda pair: (0, pair + shift))
+    half = pl.BlockSpec((tokens // 2, 128), lambda pair: (0, pair))
     whole = pl.BlockSpec((tokens, 128), lambda pair: (0, 0))
     line = pl.BlockSpec((1, 128), lambda pair: (0, 0))
     two = pl.BlockSpec((1, 2, 128), lambda pair: (pair, 0, 0))
-    low = lambda: jax.ShapeDtypeStruct((tokens, 256), jnp.bfloat16)
     wide = pltpu.VMEM((tokens, 256), jnp.bfloat16)
     both = pltpu.VMEM((2, tokens, 256), jnp.bfloat16)
     return pl.pallas_call(
@@ -712,18 +733,18 @@
             column(0),
             pl.BlockSpec((2, tokens, 128), lambda pair: (pair, 0, 0)),
             whole,
-            column(0),
-            column(0),
+            half,
+            half,
+            half,
+            half,
             whole,
             whole,
             line,
             line,
         ],
-        out_specs=[column(0), column(0), column(0), two, two],
+        out_specs=[pl.BlockSpec((3, tokens, 128), lambda pair: (0, 0, pair)), two, two],
         out_shape=[
-            low(),
-            low(),
-            low(),
+            jax.ShapeDtypeStruct((3, tokens, 256), jnp.bfloat16),
             jax.ShapeDtypeStruct((2, 2, 128), jnp.float32),
             jax.ShapeDtypeStruct((2, 2, 128), jnp.float32),
         ],
@@ -738,7 +759,7 @@
             pltpu.VMEM((tokens, 128), jnp.float32),
             pltpu.VMEM((tokens, 128), jnp.float32),
         ],
-        compiler_params=pltpu.CompilerParams(vmem_limit_bytes=48 << 20),
+        compiler_params=pltpu.CompilerParams(vmem_limit_bytes=GRANT),
         cost_estimate=pl.CostEstimate(
             flops=40 * tokens * tokens * 256,
             bytes_accessed=tokens * 256 * 40,
@@ -753,13 +774,365 @@
         values,
         extra,
         hot,
-        grads,
-        attended,
+        *grads,
+        *attended,
         cos_part,
         sin_part,
         q_gain,
         k_gain,
     )
+
+
+def front_kernel(place, *refs):
+    pieces, crossed, own, other = refs[:4], refs[4], refs[5:9], refs[9]
+    weights_out, unit_out, qkv_out = refs[10:]
+    dp_at, level, core = place[0], place[1], place[2]
+    for at_dp in range(4):
+        for at_level in range(4):
+            base = ((dp_at ^ at_dp) * 4 + (level ^ at_level)) * 64
+            mine = pl.ds(pl.multiple_of(base + core * 32, 32), 32)
+            theirs = pl.ds(pl.multiple_of(base + (1 - core) * 32, 32), 32)
+            rows = slice(at_level * 32, at_level * 32 + 32)
+            for part in range(3):
+                lanes = pl.ds(pl.multiple_of(part * 512 + core * 256, 256), 256)
+                weights_out[mine, part * 256 : (part + 1) * 256] = pieces[at_dp][rows, lanes]
+            weights_out[theirs, :] = crossed[at_dp * 128 + at_level * 32 :][:32, :]
+
+    def norm(values):
+        wide = values.astype(jnp.float32)
+        return (wide * rms_scale(wide)).astype(jnp.bfloat16)
+
+    for at in range(4):
+        unit_out[at * 128 : (at + 1) * 128, :] = norm(own[at][...])
+        unit_out[512 + at * 128 : 512 + (at + 1) * 128, :] = norm(other[at])
+    for at in range(2):
+        rows = slice(at * 512, (at + 1) * 512)
+        qkv_out[rows, :] = jnp.dot(
+            unit_out[rows, :], weights_out[...], preferred_element_type=jnp.float32
+        )
+
+
+def front(place, pieces, crossed, own, other):
+    tokens = 2 * other.shape[0] * other.shape[1]
+    quarter = pl.BlockSpec((128, 1536), lambda at: (0, 0))
+    piece = pl.BlockSpec((128, D), lambda at: (0, 0))
+    return pl.pallas_call(
+        front_kernel,
+        grid=(1,),
+        in_specs=[pl.BlockSpec(memory_space=pltpu.SMEM)]
+        + [quarter] * 4
+        + [pl.BlockSpec((512, 768), lambda at: (0, 0))]
+        + [piece] * 4
+        + [pl.BlockSpec((4, 128, D), lambda at: (0, 0, 0))],
+        out_specs=[
+            pl.BlockSpec((D, 768), lambda at: (0, 0)),
+            pl.BlockSpec((tokens, D), lambda at: (0, 0)),
+            pl.BlockSpec((tokens, 768), lambda at: (0, 0)),
+        ],
+        out_shape=[
+            jax.ShapeDtypeStruct((D, 768), jnp.bfloat16),
+            jax.ShapeDtypeStruct((tokens, D), jnp.bfloat16),
+            jax.ShapeDtypeStruct((tokens, 768), jnp.float32),
+        ],
+        compiler_params=pltpu.CompilerParams(vmem_limit_bytes=GRANT),
+        cost_estimate=pl.CostEstimate(
+            flops=2 * tokens * D * 768, bytes_accessed=12 * D * D, transcendentals=tokens
+        ),
+        name="front",
+    )(place, *pieces, crossed, *own, other)
+
+
+def place_kernel(place, *refs):
+    out, gain_out = refs[8:]
+    gain_out[...] = sum(member[128:, :128].astype(jnp.float32) for member in refs[:8])
+    dp_at, level, core = place[0], place[1], place[2]
+    for at_dp in range(4):
+        for at_level in range(4):
+            base = ((dp_at ^ at_dp) * 4 + (level ^ at_level)) * 64
+            rows = slice(at_level * 32, at_level * 32 + 32)
+            for source, side in ((refs[at_dp], core), (refs[4 + at_dp], 1 - core)):
+                to = pl.ds(pl.multiple_of(base + side * 32, 32), 32)
+                out[to, :] = source[rows, :]
+
+
+def place_rows(place, pieces, crossed):
+    quarter = pl.BlockSpec((144, D), lambda at: (0, 0))
+    return pl.pallas_call(
+        place_kernel,
+        grid=(1,),
+        in_specs=[pl.BlockSpec(memory_space=pltpu.SMEM)] + [quarter] * 8,
+        out_specs=[
+            pl.BlockSpec((D, D), lambda at: (0, 0)),
+            pl.BlockSpec((16, 128), lambda at: (0, 0)),
+        ],
+        out_shape=[
+            jax.ShapeDtypeStruct((D, D), jnp.bfloat16),
+            jax.ShapeDtypeStruct((16, 128), jnp.float32),
+        ],
+        compiler_params=pltpu.CompilerParams(vmem_limit_bytes=GRANT),
+        cost_estimate=pl.CostEstimate(flops=0, bytes_accessed=4 * D * D, transcendentals=0),
+        name="place_rows",
+    )(place, *pieces, *crossed)
+
+
+def tail_kernel(
+    place, dqkv, weights, unit, gains, biases, ffn_gain, back_kept, back_sent, kept, sent, part, small
+):
+    core, group = place[2], place[3]
+    tokens = unit.shape[0]
+
+    def back(rows):
+        total = contract_last(dqkv[0, rows, :], weights[:, :256])
+        for at in (1, 2):
+            total += contract_last(dqkv[at, rows, :], weights[:, at * 256 : (at + 1) * 256])
+        return total
+
+    back_kept[...] = back(slice(0, tokens // 2))
+    back_sent[...] = back(slice(tokens // 2, tokens)).astype(jnp.bfloat16)
+    for at in range(3):
+        part[:, at * 256 : (at + 1) * 256] = rows_inner(unit[...], dqkv[at]).astype(jnp.bfloat16)
+    for at in range(16):
+        rows = slice(at * 32, at * 32 + 32)
+        kept[rows, :] = part[pl.ds(pl.multiple_of(at * 64 + core * 32, 32), 32), :]
+        sent[rows, :] = part[pl.ds(pl.multiple_of(at * 64 + (1 - core) * 32, 32), 32), :]
+    lane = lax.broadcasted_iota(jnp.int32, (1, 128), 1)
+    sums = gains[0] + gains[1]
+    sums = sums + pltpu.roll(sums, HD, 1)
+    placed = jnp.zeros((1, 128), jnp.float32)
+    for head in range(4):
+        line = biases[head // 2, head % 2 : head % 2 + 1, :]
+        same = jnp.sum(jnp.where(lane < 8, line, 0.0), axis=1, keepdims=True)
+        total = jnp.sum(jnp.where(lane == LSE_LANE, line, 0.0), axis=1, keepdims=True)
+        spot = group * 4 + head
+        placed = jnp.where(lane == spot, same, placed)
+        placed = jnp.where(lane == spot + H, total - same, placed)
+    small[...] = jnp.zeros(small.shape, jnp.float32)
+    for at in range(4):
+        small[at : at + 1, :256] = ffn_gain[:, at * 256 : (at + 1) * 256]
+    small[4:5, :128] = jnp.where(lane < HD, sums[0:1], sums[1:2])
+    small[4:5, 128:256] = placed
+    kept[512:, :] = small[...].astype(jnp.bfloat16)
+    sent[512:, :] = small[...].astype(jnp.bfloat16)
+
+
+def tail(place, dqkv, weights, unit, gains, biases, ffn_gain):
+    tokens = unit.shape[0]
+    whole = lambda shape: pl.BlockSpec(shape, lambda at: (0,) * len(shape))
+    shapes = [
+        ((tokens // 2, D), jnp.float32),
+        ((tokens // 2, D), jnp.bfloat16),
+        ((528, 768), jnp.bfloat16),
+        ((528, 768), jnp.bfloat16),
+    ]
+    arguments = (dqkv, weights, unit, gains, biases, ffn_gain)
+    return pl.pallas_call(
+        tail_kernel,
+        grid=(1,),
+        in_specs=[pl.BlockSpec(memory_space=pltpu.SMEM)]
+        + [whole(member.shape) for member in arguments],
+        out_specs=[whole(shape) for shape, _ in shapes],
+        out_shape=[jax.ShapeDtypeStruct(shape, kind) for shape, kind in shapes],
+        scratch_shapes=[pltpu.VMEM((D, 768), jnp.bfloat16), pltpu.VMEM((16, 768), jnp.float32)],
+        compiler_params=pltpu.CompilerParams(vmem_limit_bytes=GRANT),
+        cost_estimate=pl.CostEstimate(
+            flops=4 * tokens * D * 768, bytes_accessed=14 * D * D, transcendentals=0
+        ),
+        name="tail",
+    )(place, *arguments)
+
+
+def lower_kernel(gate, up, down, out):
+    out[0] = gate[...].astype(jnp.bfloat16)
+    out[1] = up[...].astype(jnp.bfloat16)
+    out[2] = down[...].astype(jnp.bfloat16)
+
+
+def lower(gate, up, down):
+    whole = pl.BlockSpec(gate.shape, lambda at: (0, 0))
+    return pl.pallas_call(
+        lower_kernel,
+        grid=(1,),
+        in_specs=[whole] * 3,
+        out_specs=pl.BlockSpec((3,) + gate.shape, lambda at: (0, 0, 0)),
+        out_shape=jax.ShapeDtypeStruct((3,) + gate.shape, jnp.bfloat16),
+        compiler_params=pltpu.CompilerParams(vmem_limit_bytes=GRANT),
+        name="lower",
+    )(gate, up, down)
+
+
+def middle_back_kernel(
+    kept, near, side, far, dy_in, middle_in, gain_in, weights, grad_out, low_out, att_out, sums_out
+):
+    wide = jnp.float32
+    upstream = (kept[...] + near[...].astype(wide)) + (
+        side[...].astype(wide) + far[...].astype(wide)
+    )
+    middle = middle_in[...]
+    inv = rms_scale(middle)
+    sums_out[...] = jnp.sum(upstream * middle * inv, axis=0, keepdims=True)
+    grad = dy_in[...].astype(wide) + norm_back(middle, inv, gain_in[...], upstream)
+    grad_out[...] = grad
+    grad_low = grad.astype(jnp.bfloat16)
+    low_out[...] = grad_low
+    att_out[...] = contract_last(grad_low, weights[...]).astype(jnp.bfloat16)
+
+
+def middle_back(kept, moved, own_dy, middle, gain_two, w_out):
+    rows = kept.shape[0]
+    block = pl.BlockSpec((rows, D), lambda at: (0, 0))
+    line = pl.BlockSpec((1, D), lambda at: (0, 0))
+    return pl.pallas_call(
+        middle_back_kernel,
+        grid=(1,),
+        in_specs=[block] * 6 + [line, pl.BlockSpec((D, D), lambda at: (0, 0))],
+        out_specs=[block, block, block, line],
+        out_shape=[
+            jax.ShapeDtypeStruct((rows, D), jnp.float32),
+            jax.ShapeDtypeStruct((rows, D), jnp.bfloat16),
+            jax.ShapeDtypeStruct((rows, D), jnp.bfloat16),
+            jax.ShapeDtypeStruct((1, D), jnp.float32),
+        ],
+        compiler_params=pltpu.CompilerParams(vmem_limit_bytes=GRANT),
+        cost_estimate=pl.CostEstimate(
+            flops=2 * rows * D * D, bytes_accessed=22 * rows * D + 2 * D * D, transcendentals=rows
+        ),
+        name="middle_back",
+    )(kept, *moved, own_dy, middle, gain_two, w_out)
+
+
+GATED = 512
+HIDDEN = 256
+
+
+def gated_kernel(count, *refs):
+    tokens_in, grads_in, weights = refs[:count], refs[count : 2 * count], refs[2 * count]
+    hidden_out, back_out = refs[2 * count + 1 : 3 * count + 1], refs[3 * count + 1 : 4 * count + 1]
+    totals = refs[4 * count + 1 :]
+    step = pl.program_id(0)
+    pair = weights[0:2].reshape(2 * GATED, D)
+    for at in range(count):
+        both = contract_last(tokens_in[at][...], pair)
+        gate, up = both[:, :GATED], both[:, GATED:]
+        grad_hidden = contract_last(grads_in[at][...], weights[2])
+        sig = lax.logistic(gate)
+        swished = gate * sig
+        hidden_out[at][2] = (swished * up).astype(jnp.bfloat16)
+        grad_gate = (grad_hidden * up * sig * (1.0 + gate * (1.0 - sig))).astype(jnp.bfloat16)
+        grad_up = (grad_hidden * swished).astype(jnp.bfloat16)
+        hidden_out[at][0] = grad_gate
+        hidden_out[at][1] = grad_up
+        added = jnp.dot(
+            jnp.concatenate([grad_gate, grad_up], axis=1), pair, preferred_element_type=jnp.float32
+        )
+        total = totals[at]
+
+        @pl.when(step == 0)
+        def _():
+            total[...] = added
+
+        @pl.when(step == pl.num_programs(0) - 1)
+        def _():
+            back_out[at][...] = (total[...] + added).astype(back_out[at].dtype)
+
+
+def gated(tokens_in, grads_in, weights, kind):
+    count = len(tokens_in)
+    chunk = tokens_in[0].shape[0]
+    hidden = weights.shape[1]
+    assert hidden == 2 * GATED
+    whole = pl.BlockSpec((chunk, D), lambda at: (0, 0))
+    results = pl.pallas_call(
+        functools.partial(gated_kernel, count),
+        grid=(2,),
+        in_specs=[whole] * (2 * count) + [pl.BlockSpec((3, GATED, D), lambda at: (0, at, 0))],
+        out_specs=[pl.BlockSpec((3, chunk, GATED), lambda at: (0, 0, at))] * count
+        + [whole] * count,
+        out_shape=[jax.ShapeDtypeStruct((3, chunk, hidden), jnp.bfloat16)] * count
+        + [jax.ShapeDtypeStruct((chunk, D), kind)] * count,
+        scratch_shapes=[pltpu.VMEM((chunk, D), jnp.float32)] * count,
+        compiler_params=pltpu.CompilerParams(vmem_limit_bytes=GRANT),
+        cost_estimate=pl.CostEstimate(
+            flops=10 * count * chunk * D * hidden,
+            bytes_accessed=2 * D * (7 * count * chunk + 3 * hidden),
+            transcendentals=count * chunk * hidden,
+        ),
+        name="gated",
+    )(*tokens_in, *grads_in, weights)
+    return list(zip(results[:count], results[count:]))
+
+
+def ffn_grads_kernel(*refs):
+    tokens_in, grads_in, hidden_in = refs[0:4], refs[4:8], refs[8:12]
+    grads_out, tokens_all, grads_all, hidden = refs[12:]
+    chunk = tokens_in[0].shape[0]
+    rows_of = [slice(at * chunk, (at + 1) * chunk) for at in range(4)]
+
+    @pl.when(pl.program_id(0) == 0)
+    def _():
+        for at in range(4):
+            tokens_all[rows_of[at], :] = tokens_in[at][...]
+            grads_all[rows_of[at], :] = grads_in[at][...]
+
+    for which in range(3):
+        for at in range(4):
+            hidden[which, rows_of[at], :] = hidden_in[at][which]
+        other = tokens_all if which < 2 else grads_all
+        grads_out[which] = rows_inner(hidden[which], other[...]).astype(jnp.bfloat16)
+
+
+def ffn_grads(tokens_in, grads_in, hidden_in):
+    chunk = tokens_in[0].shape[0]
+    tokens = 4 * chunk
+    hidden = hidden_in[0].shape[2]
+    whole = pl.BlockSpec((chunk, D), lambda at: (0, 0))
+    wide_low = pltpu.VMEM((tokens, D), jnp.bfloat16)
+    return pl.pallas_call(
+        ffn_grads_kernel,
+        grid=(hidden // HIDDEN,),
+        in_specs=[whole] * 8 + [pl.BlockSpec((3, chunk, HIDDEN), lambda at: (0, 0, at))] * 4,
+        out_specs=pl.BlockSpec((3, HIDDEN, D), lambda at: (0, at, 0)),
+        out_shape=jax.ShapeDtypeStruct((3, hidden, D), jnp.bfloat16),
+        scratch_shapes=[wide_low, wide_low, pltpu.VMEM((3, tokens, HIDDEN), jnp.bfloat16)],
+        compiler_params=pltpu.CompilerParams(vmem_limit_bytes=GRANT),
+        cost_estimate=pl.CostEstimate(
+            flops=6 * tokens * D * hidden,
+            bytes_accessed=2 * D * (4 * tokens + 6 * hidden),
+            transcendentals=0,
+        ),
+        name="ffn_grads",
+    )(*tokens_in, *grads_in, *hidden_in)
+
+
+def down_kernel(*refs):
+    hidden_in, weights = refs[:4], refs[4]
+    outs = refs[5:]
+    for at in range(4):
+        outs[at][...] = jnp.dot(
+            hidden_in[at][0], weights[0], preferred_element_type=jnp.float32
+        ).astype(outs[at].dtype)
+
+
+def down(hidden_in, weights):
+    chunk = hidden_in[0].shape[1]
+    hidden = weights.shape[1]
+    half = D // 2
+    block = pl.BlockSpec((chunk, half), lambda at: (0, at))
+    return pl.pallas_call(
+        down_kernel,
+        grid=(2,),
+        in_specs=[pl.BlockSpec((1, chunk, hidden), lambda at: (2, 0, 0))] * 4
+        + [pl.BlockSpec((1, hidden, half), lambda at: (2, 0, at))],
+        out_specs=[block] * 4,
+        out_shape=[jax.ShapeDtypeStruct((chunk, D), jnp.float32)]
+        + [jax.ShapeDtypeStruct((chunk, D), jnp.bfloat16)] * 3,
+        compiler_params=pltpu.CompilerParams(vmem_limit_bytes=GRANT),
+        cost_estimate=pl.CostEstimate(
+            flops=8 * chunk * D * hidden,
+            bytes_accessed=2 * D * (9 * chunk + hidden),
+            transcendentals=0,
+        ),
+        name="down",
+    )(*hidden_in, weights)
 
 
 def local_split(
@@ -790,54 +1163,65 @@
     parity = level & 1
     piece = inputs.shape[2]
     tokens = 8 * piece
+    others = (1, 2, 3)
     swap_core = lambda values: swap_seq(values, 1)
     swap_level = lambda values, mask: swap_seq(values, 2 * mask)
 
-    def gather_sequence(pair):
-        mine = at_index(pair, batch)
-        other = at_index(pair, 1 - batch)
-        far = swap_level(other, 2)
-        near = swap_level(mine, 1)
-        last = swap_level(far, 1)
-        four = jnp.stack([mine, near, far, last])
-        return jnp.stack([four, swap_core(four)])
-
-    own_x = inputs[:, 0]
-    ids = gather_sequence(jnp.stack([variate_ids[:, 0], time_ids[:, 0]], axis=1))
-    sequence = gather_sequence(own_x).reshape(tokens, D)
+    own_dy = out_grad[:, 0].reshape(2 * piece, D)
 
     gain_low = attn_gain.astype(low).astype(wide)
     weights_low = jnp.stack([query_weight, key_weight, value_weight], axis=1).astype(low)
     scaled = (weights_low.astype(wide) * gain_low[:, None, None]).astype(low)
-    scaled = scaled.reshape(32, 3, 2, 2, 256)
-    rows = ordered(
-        [at_index(scaled, core, 3), swap_core(at_index(scaled, 1 - core, 3))], core
-    ).reshape(64, 3, 2, 256)
-    same = at_index(rows, parity, 2).reshape(64, 768)
-    cross = at_index(rows, 1 - parity, 2).reshape(64, 768)
-    rows = ordered(
-        [same, swap_level(cross, 1), swap_level(same, 2), swap_level(cross, 3)], level
-    ).reshape(256, 768)
-    w_qkv = ordered([rows] + [swap_dp(rows, mask) for mask in (1, 2, 3)], dp_at).reshape(D, 768)
-
+    scaled = scaled.reshape(32, 3, 2, 512)
+    kinds = variate_ids[:, 0]
+    times = time_ids[:, 0]
+    ids = jnp.stack([kinds, times // 64, times % 64], axis=1).astype(low)
+    ids = jnp.concatenate([ids, swap_core(ids)], axis=1)
+    ids = jnp.pad(ids, ((0, 0), (0, 26), (0, 0)))
+
+    def with_ids(weights_part, which):
+        return jnp.concatenate(
+            [weights_part.reshape(32, 1536), at_index(ids, which)], axis=1
+        )
+
+    same = with_ids(at_index(scaled, parity, 2), 1 - batch)
+    cross_near = with_ids(at_index(scaled, 1 - parity, 2), batch)
+    cross_far = with_ids(at_index(scaled, 1 - parity, 2), 1 - batch)
+    moved = [swap_level((cross_near, same, cross_far)[mask - 1], mask) for mask in others]
+    own_x = inputs[:, 0]
+    near, far = at_index(own_x, batch), at_index(own_x, 1 - batch)
     with_gain = jnp.concatenate(
-        [out_weight.astype(low), jnp.pad(ffn_gain.astype(low)[:, None], ((0, 0), (0, 127)))], axis=1
-    )
-    rows = ordered([with_gain] + [swap_level(with_gain, mask) for mask in (1, 2, 3)], level)
-    rows = ordered([rows] + [swap_dp(rows, mask) for mask in (1, 2, 3)], dp_at)
-    w_out = ordered([rows, swap_core(rows)], core)
-    w_out = jnp.transpose(w_out, (1, 2, 0, 3, 4)).reshape(D, D + 128)
-    gain_two = w_out[:, D].astype(wide)[None, :]
-    w_out = w_out[:, :D]
-
-    own_dy = out_grad[:, 0].reshape(2 * piece, D)
-    all_dy = jnp.concatenate([own_dy] + [swap_dp(own_dy, mask) for mask in (1, 2, 3)])
-
-    ffn_local = jnp.stack([gate_weight, up_weight, down_weight]).astype(low)
-    w_ffn = lax.all_gather(ffn_local, "seq", axis=1, tiled=True)
+        [
+            out_weight.astype(low).reshape(32, D),
+            jnp.where(
+                jnp.arange(16)[:, None] == dp_at * 4 + level,
+                jnp.where(
+                    core == 0,
+                    jnp.pad(ffn_gain.astype(low)[None, :], ((0, 0), (0, D - 32))),
+                    jnp.pad(ffn_gain.astype(low)[None, :], ((0, 0), (32, D - 64))),
+                ),
+                0.0,
+            ).astype(low),
+        ]
+    )
+    near = jnp.concatenate([near, with_gain])
+    far = jnp.concatenate([far, with_gain])
+    same, near, far, gate_local, up_local, down_local, *moved = together(
+        same, near, far, gate_weight, up_weight, down_weight, *moved
+    )
+
+    place = jnp.stack([dp_at, level, core, 2 * parity + core]).astype(jnp.int32)
+    rows = jnp.concatenate([same[:, :1536]] + [member[:, :1536] for member in moved])
+    ids = jnp.stack([at_index(ids, batch)] + [member[:, 1536:] for member in moved])
+    moved = [swap_dp(rows, mask) for mask in others]
+    from_far = swap_level(far, 2)
+    from_near = swap_level(near, 1)
+    ffn_local = lower(gate_local, up_local, down_local)
+    last = swap_level(from_far, 1)
+    ids = jnp.stack([ids[:, :3], ids[:, 3:6]]).astype(wide)
 
     kinds = ids[:, :, 0].reshape(tokens, 1)
-    times = ids[:, :, 1].reshape(tokens, 1).astype(wide)
+    times = (ids[:, :, 1] * 64.0 + ids[:, :, 2]).reshape(tokens, 1)
     lane = lax.broadcasted_iota(jnp.int32, (1, 128), 1)
     hot = jnp.where(
         lane < LSE_LANE, (kinds == lane % 8).astype(wide), jnp.where(lane < LSE_LANE + 3, 1.0, 0.0)
@@ -860,137 +1244,241 @@
         ),
     ).reshape(2, 2, 128)
 
-    seq_wide = sequence.astype(wide)
-    unit = (seq_wide * rms_scale(seq_wide)).astype(low)
-    qkv = product(unit, w_qkv)
-    attended, *saved = attend(qkv, cos_part, sin_part, hot, q_gain, k_gain, bias_rows)
-
-    parts = attended.reshape(2, 4, piece, 256)
-    both = jnp.stack([parts[0], swap_core(parts[1])], axis=2)
-    arrived = [both[0]] + [swap_level(both[mask], mask) for mask in (1, 2, 3)]
-    split = jnp.stack(arrived).reshape(2, 2, piece, 2, 256)
-    split = jnp.where(batch == 1, split[::-1], split)
-    split = jnp.where(parity == 1, split[:, ::-1], split)
-    split = jnp.where(core == 1, split[:, :, :, ::-1], split)
-    own_att = jnp.transpose(split, (0, 2, 1, 3, 4)).reshape(2 * piece, D)
+    rows, ffn_local, near, from_near, from_far, last, cos_part, sin_part, dy_sent, *moved = together(
+        rows, ffn_local, near, from_near, from_far, last, cos_part, sin_part, own_dy, *moved
+    )
+    w_ffn = lax.all_gather(ffn_local, "seq", axis=1, tiled=True)
+
+    pieces = [rows] + moved
+    four = [near, from_near, from_far, last]
+    own = [member[:piece] for member in four]
+    tiles = [member[piece + 32 :] for member in four]
+    out_rows = jnp.concatenate(
+        [member[piece : piece + 32] for member in four]
+        + [(tiles[0] + tiles[1]) + (tiles[2] + tiles[3])]
+    )
+    sent = jnp.concatenate(
+        [
+            jnp.concatenate(
+                [
+                    jnp.where(
+                        core == 0,
+                        member[:, at * 512 + 256 : at * 512 + 512],
+                        member[:, at * 512 : at * 512 + 256],
+                    )
+                    for at in range(3)
+                ],
+                axis=1,
+            )
+            for member in pieces
+        ]
+    )
+    crossed, rows_crossed, out_rows, dy_sent = together(
+        swap_core(jnp.stack(own)), swap_core(sent), out_rows, dy_sent
+    )
+
+    w_qkv, unit, qkv = front(place, pieces, rows_crossed, four, crossed)
+    att_near, att_far, *saved = attend(qkv, cos_part, sin_part, hot, q_gain, k_gain, bias_rows)
+    attended = (att_near, att_far)
+    att_near, att_far, dy_near, dy_side, *pieces = together(
+        att_near,
+        att_far,
+        swap_dp(dy_sent, 1),
+        swap_dp(dy_sent, 2),
+        out_rows,
+        *[swap_dp(out_rows, mask) for mask in others],
+    )
+
+    part, crossed, *rows_crossed = together(
+        att_near, swap_core(att_far), *[swap_core(member) for member in pieces]
+    )
+    part, crossed = part.reshape(4, piece, 256), crossed.reshape(4, piece, 256)
+    both = jnp.concatenate(
+        [jnp.where(core == 0, part, crossed), jnp.where(core == 0, crossed, part)], axis=2
+    )
+
+    w_out, gain_two = place_rows(place, pieces, rows_crossed)
+    w_out, gain_two, dy_far, *arrived = together(
+        w_out,
+        gain_two,
+        swap_dp(dy_sent, 3),
+        both[0],
+        *[swap_level(both[mask], mask) for mask in others],
+    )
+    gain_two = gain_two[:, :64].reshape(1, D)
+    blocks = [pick(arrived, level ^ at) for at in range(4)]
+    own_att = jnp.concatenate(
+        [
+            jnp.concatenate([blocks[0], blocks[1]], axis=1),
+            jnp.concatenate([blocks[2], blocks[3]], axis=1),
+        ]
+    )
 
     own_wide = own_x.reshape(2 * piece, D).astype(wide)
     middle = own_wide + product(own_att, w_out)
     inv_two = rms_scale(middle)
     normed_two = (middle * inv_two * gain_two).astype(low)
-    all_two = jnp.concatenate([normed_two] + [swap_dp(normed_two, mask) for mask in (1, 2, 3)])
-
-    w_gate, w_up, w_down = w_ffn[0], w_ffn[1], w_ffn[2]
-    gate_pre = times_transposed(all_two, w_gate)
-    up_pre = times_transposed(all_two, w_up)
-    grad_hidden = times_transposed(all_dy, w_down)
-    gate_sig = jax.nn.sigmoid(gate_pre)
-    hidden = (gate_pre * gate_sig * up_pre).astype(low)
-    grad_gate = (grad_hidden * up_pre * gate_sig * (1.0 + gate_pre * (1.0 - gate_sig))).astype(low)
-    grad_up = (grad_hidden * gate_pre * gate_sig).astype(low)
-
-    def scatter_tokens(partial):
-        chunks = partial.reshape(4, 2 * piece, D)
-        total = chunks[0]
-        for mask in (1, 2, 3):
-            total = total + swap_dp(chunks[mask].astype(low), mask).astype(wide)
-        return total
-
-    grad_two = scatter_tokens(product(grad_gate, w_gate) + product(grad_up, w_up))
-    result = middle + scatter_tokens(product(hidden, w_down))
-    ffn_grads = jnp.stack(
-        [
-            rows_inner(grad_gate, all_two).astype(low),
-            rows_inner(grad_up, all_two).astype(low),
-            rows_inner(hidden, all_dy).astype(low),
-        ]
-    )
-    ffn_grads = lax.psum_scatter(ffn_grads, "seq", scatter_dimension=1, tiled=True).astype(wide)
-
-    dy_wide = own_dy.astype(wide)
-    gain_two_part = jnp.sum(grad_two * middle * inv_two, axis=0)
-    grad_middle = dy_wide + norm_back(middle, inv_two, gain_two, grad_two)
-    middle_low = grad_middle.astype(low)
-    grad_att = times_transposed(middle_low, w_out).astype(low)
-    out_part = rows_inner(own_att, middle_low)
-
-    split = jnp.transpose(grad_att.reshape(2, piece, 2, 2, 256), (0, 2, 1, 3, 4))
-    split = jnp.where(batch == 1, split[::-1], split)
-    split = jnp.where(parity == 1, split[:, ::-1], split)
-    split = jnp.where(core == 1, split[:, :, :, ::-1], split)
-    split = split.reshape(4, piece, 2, 256)
-    arrived = jnp.stack([split[0]] + [swap_level(split[mask], mask) for mask in (1, 2, 3)])
-    grads = jnp.stack([arrived[:, :, 0], swap_core(arrived[:, :, 1])]).reshape(tokens, 256)
-
-    dq, dk, dv, gain_sums, bias_sums = attend_back(
+    dy_pieces = [own_dy, dy_near, dy_side, dy_far]
+
+    own_two, w_ffn, middle, *dy_pieces = together(normed_two, w_ffn, middle, *dy_pieces)
+    ((own_hidden, kept),) = gated([own_two], dy_pieces[:1], w_ffn, wide)
+    own_two, near_two, side_two, own_hidden, kept = together(
+        own_two, swap_dp(own_two, 1), swap_dp(own_two, 2), own_hidden, kept
+    )
+
+    (near_hidden, near_back), (side_hidden, side_back) = gated(
+        [near_two, side_two], dy_pieces[1:3], w_ffn, low
+    )
+    far_two, near_hidden, near_back, side_hidden, side_back = together(
+        swap_dp(own_two, 3), near_hidden, near_back, side_hidden, side_back
+    )
+
+    near_back, side_back = swap_dp(near_back, 1), swap_dp(side_back, 2)
+    ((far_hidden, far_back),) = gated([far_two], dy_pieces[3:], w_ffn, low)
+    far_hidden, far_back = together(far_hidden, far_back)
+    hidden = [own_hidden, near_hidden, side_hidden, far_hidden]
+    ffn_part = ffn_grads([own_two, near_two, side_two, far_two], dy_pieces, hidden)
+    ffn_part, kept, *moved = together(
+        ffn_part, kept, near_back, side_back, swap_dp(far_back, 3)
+    )
+    ffn_shard = lax.psum_scatter(ffn_part, "seq", scatter_dimension=1, tiled=True)
+    grad_middle, middle_low, grad_att, gain_two_part = middle_back(
+        kept, moved, own_dy, middle, gain_two, w_out
+    )
+
+    blocks = [
+        grad_att[at // 2 * piece : (at // 2 + 1) * piece, at % 2 * 512 : (at % 2 + 1) * 512]
+        for at in range(4)
+    ]
+    arrived = [pick(blocks, level)]
+    arrived += [swap_level(pick(blocks, level ^ mask), mask) for mask in others]
+    out_part = rows_inner(own_att, middle_low).astype(low).reshape(4, 4, 2, 32, D)
+    out_kept = at_index(out_part, core, 2)
+    out_crossed = swap_core(at_index(out_part, 1 - core, 2))
+    down_kept, *down_chunks = down(hidden, w_ffn)
+    out_kept, out_crossed, down_kept, *rest = together(
+        out_kept, out_crossed, down_kept, *down_chunks, *arrived
+    )
+    down_chunks, arrived = rest[:3], rest[3:]
+
+    halves = [
+        jnp.concatenate([member[:, :256] for member in arrived]),
+        jnp.concatenate([member[:, 256:] for member in arrived]),
+    ]
+    out_half = (out_kept.astype(wide) + out_crossed.astype(wide)).astype(low)
+    kept, crossed, out_half, *down_chunks = together(
+        pick(halves, core), swap_core(pick(halves, 1 - core)), out_half, *down_chunks
+    )
+    grads = (kept, crossed)
+
+    out_moved = [swap_dp(at_index(out_half, dp_at ^ mask), mask) for mask in others]
+    down_moved = [swap_dp(down_chunks[mask - 1], mask) for mask in (1, 2)]
+    dqkv, gain_sums, bias_sums = attend_back(
         qkv, saved, hot, grads, attended, cos_part, sin_part, q_gain, k_gain
     )
-    dqkv = jnp.concatenate([dq, dk, dv], axis=1)
-
-    qkv_part = rows_inner(unit, dqkv).astype(low).reshape(4, 4, 2, 32, 768)
-    other = swap_core(at_index(qkv_part, 1 - core, 2))
-    qkv_part = jnp.stack([at_index(qkv_part, core, 2), other], axis=2)
-    total = at_index(qkv_part, dp_at).astype(wide)
-    for mask in (1, 2, 3):
-        total = total + swap_dp(at_index(qkv_part, dp_at ^ mask), mask).astype(wide)
-    total = total.astype(low)
-    same = at_index(total, level).astype(wide) + swap_level(at_index(total, level ^ 2), 2).astype(
-        wide
-    )
-    cross = swap_level(at_index(total, level ^ 1), 1).astype(wide) + swap_level(
-        at_index(total, level ^ 3), 3
-    ).astype(wide)
-    split = jnp.stack([same, cross]).reshape(2, 2, 32, 3, 256)
-    split = jnp.where(parity == 1, split[::-1], split)
-    split = jnp.where(core == 1, split[:, ::-1], split)
-    unit_grads = jnp.transpose(split, (3, 2, 0, 1, 4)).reshape(3, 32, D)
-    gain_grad = jnp.sum(unit_grads * jnp.transpose(weights_low, (1, 0, 2)).astype(wide), axis=(0, 2))
-    qkv_grads = unit_grads * gain_low[None, :, None]
-
-    unit_back = times_transposed(dqkv, w_qkv).reshape(2, 4, piece, D)
-    total = unit_back[0] + swap_core(unit_back[1].astype(low)).astype(wide)
-    passed = total[2] + swap_level(total[3].astype(low), 1).astype(wide)
-    kept = total[0] + swap_level(total[1].astype(low), 1).astype(wide)
-    passed = swap_level(passed.astype(low), 2).astype(wide)
-    back = jnp.stack([kept, passed])
-    back = jnp.where(batch == 1, back[::-1], back).reshape(2 * piece, D)
+    dqkv, last_chunk, *rest = together(dqkv, down_chunks[2], *out_moved, *down_moved)
+    out_moved = [member.astype(wide) for member in rest[:3]]
+    out_sum = (at_index(out_half, dp_at).astype(wide) + out_moved[0]) + (out_moved[1] + out_moved[2])
+    down_moved = rest[3:]
+
+    back_kept, back_sent, kept, sent = tail(
+        place, dqkv, w_qkv, unit, gain_sums, bias_sums, gain_two_part
+    )
+    back_kept, back_crossed, kept, crossed = together(
+        back_kept, swap_core(back_sent), kept, swap_core(sent)
+    )
+
+    back = (back_kept + back_crossed.astype(wide)).reshape(4, piece, D)
+    small_low = (kept[512:].astype(wide) + crossed[512:].astype(wide)).astype(low)
+
+    def dp_message(to):
+        return jnp.concatenate(
+            [
+                lax.dynamic_slice_in_dim(kept, to * 128, 128),
+                lax.dynamic_slice_in_dim(crossed, to * 128, 128),
+                small_low,
+            ]
+        )
+
+    moved = [swap_dp(dp_message(dp_at ^ mask), mask) for mask in others]
+    back_low = back.astype(low)
+    back_moved = [swap_level(back_low[mask], mask) for mask in (2, 3)]
+    qkv_kept, kept, near, ffn_shard, middle, down_kept, last_chunk, *rest = together(
+        dp_message(dp_at),
+        back[0],
+        back_low[1],
+        ffn_shard,
+        middle,
+        down_kept,
+        last_chunk,
+        *down_moved,
+        *back_moved,
+        *moved,
+    )
+    down_moved = rest[:2]
+    back_moved = [member.astype(wide) for member in rest[2:4]]
+    moved = rest[4:]
+    ffn_sums = ffn_shard.astype(wide)
+
+    moved = [member.astype(wide) for member in moved]
+    total = qkv_kept.astype(wide)
+    total = ((total + moved[0]) + (moved[1] + moved[2])).astype(low)
+    small_low = total[256:]
+
+    def level_message(to):
+        out_block = at_index(out_sum, to).astype(low)
+        qkv_block = jnp.concatenate(
+            [
+                lax.dynamic_slice_in_dim(total, to * 32, 32),
+                lax.dynamic_slice_in_dim(total, 128 + to * 32, 32),
+            ]
+        )
+        return jnp.concatenate(
+            [qkv_block[:, at * 256 : (at + 1) * 256] for at in range(3)]
+            + [out_block[:, at * 256 : (at + 1) * 256] for at in range(4)]
+            + [small_low[:, :256]]
+        )
+
+    moved = [swap_level(level_message(level ^ mask), mask) for mask in others]
+    passed = back_moved[0] + back_moved[1]
+    mine, kept, passed, near, last_chunk, *moved = together(
+        level_message(level), kept, passed, swap_level(near, 1), swap_dp(last_chunk, 3), *moved
+    )
+    kept = kept + near.astype(wide)
+    down_moved = [member.astype(wide) for member in down_moved + [last_chunk]]
+    result = middle + ((down_kept + down_moved[0]) + (down_moved[1] + down_moved[2]))
+    result = result.astype(low)
+    moved = [member.astype(wide) for member in moved]
+    mine = mine.astype(wide)
+    back = jnp.concatenate(
+        [jnp.where(batch == 0, kept, passed), jnp.where(batch == 0, passed, kept)]
+    )
     inv_one = rms_scale(own_wide)
     inner = jnp.mean(back * own_wide, axis=-1, keepdims=True)
     input_grad = grad_middle + inv_one * back - own_wide * (inv_one * inv_one * inv_one) * inner
-
-    out_part = out_part.reshape(4, 4, 2, 32, D)
-    total = at_index(out_part, core, 2) + swap_core(
-        at_index(out_part, 1 - core, 2).astype(low)
-    ).astype(wide)
-    kept = at_index(total, dp_at)
-    for mask in (1, 2, 3):
-        kept = kept + swap_dp(at_index(total, dp_at ^ mask).astype(low), mask).astype(wide)
-    out_grads = at_index(kept, level)
-    for mask in (1, 2, 3):
-        out_grads = out_grads + swap_level(
-            at_index(kept, level ^ mask).astype(low), mask
-        ).astype(wide)
-
-    gain_sums = jnp.sum(gain_sums, axis=0).reshape(2, 2, HD)
-    gain_sums = jnp.sum(gain_sums, axis=1).reshape(128)
-    bias_sums = bias_sums.reshape(4, 128)
-    same = jnp.sum(bias_sums[:, :8], axis=1)
-    pair = jnp.stack([same, bias_sums[:, LSE_LANE] - same])
-    placed = jnp.where(jnp.arange(4)[None, :, None] == group, pair[:, None, :], 0.0).reshape(2 * H)
-    small = jnp.concatenate([gain_two_part, gain_sums, placed, jnp.zeros((96,), wide)])
-    small = small.reshape(10, 128)
-    for swap, masks in ((swap_dp, (1, 2, 3)), (swap_level, (1, 2, 3)), (swap_seq, (1,))):
-        moved = [small] + [swap(small, mask) for mask in masks]
-        while len(moved) > 1:
-            moved = [left + right for left, right in zip(moved[::2], moved[1::2])]
-        small = moved[0]
-    small = small.reshape(1280)
+    input_grad = input_grad.astype(low)
+
+    small = (mine[320:] + moved[0][320:]) + (moved[1][320:] + moved[2][320:])
+    small = small[:5].reshape(1280)
+    out_grads = (mine[192:320] + moved[0][192:320]) + (moved[1][192:320] + moved[2][192:320])
+    out_grads = jnp.concatenate([out_grads[at * 32 : (at + 1) * 32] for at in range(4)], axis=1)
+    same = (mine[:192] + moved[1][:192]).reshape(3, 2, 32, 256)
+    cross = (moved[0][:192] + moved[2][:192]).reshape(3, 2, 32, 256)
+    quarters = []
+    for member in (jnp.where(parity == 0, same, cross), jnp.where(parity == 0, cross, same)):
+        quarters += [
+            jnp.where(core == 0, member[:, 0], member[:, 1]),
+            jnp.where(core == 0, member[:, 1], member[:, 0]),
+        ]
+    unit_grads = jnp.concatenate(quarters, axis=2)
     gain_two_grad = lax.dynamic_slice_in_dim(small, (dp_at * 8 + seq_at) * 32, 32)
+    gain_grad = jnp.sum(unit_grads * jnp.transpose(weights_low, (1, 0, 2)).astype(wide), axis=(0, 2))
+    qkv_grads = unit_grads * gain_low[None, :, None]
 
     shape = (2, 1, piece, D)
     return (
-        result.astype(low).reshape(shape),
-        input_grad.astype(low).reshape(shape),
+        result.reshape(shape),
+        input_grad.reshape(shape),
         gain_grad,
         qkv_grads[0],
         qkv_grads[1],
@@ -1000,9 +1488,9 @@
         small[D + HD : D + 2 * HD],
         small[D + 2 * HD : D + 2 * HD + 2 * H].reshape(2, H),
         gain_two_grad,
-        ffn_grads[0],
-        ffn_grads[1],
-        ffn_grads[2],
+        ffn_sums[0],
+        ffn_sums[1],
+        ffn_sums[2],
     )
 
 

time: 453 us -> 350 us (0.77)
  waiting for transfers between devices: 181 us -> 100 us
  Pallas kernels: 33.3 us -> 105 us
  matrix products: 47.2 us -> 4.17 us
  other arithmetic: 54.3 us -> 30.9 us
  local copies, waits for them, and re-layouts: 40.1 us -> 19.4 us
    ppermute x27 -> x24, waiting for transfers between devices: 90 us -> 20.4 us  [swap_dp(): return lax.ppermute(values, 'dp', [(at, at ^ mask) for at in range(4)])]
    pallas_call x0 -> x10, Pallas kernels: none -> 67.6 us  [the longest x3 25.4 us: gated(): pl.pallas_call(functools.partial(gated_kernel, count), grid=(2,), in_spec...]
    dot_general x5 -> x0, matrix products: 18.1 us -> none  [times_transposed(): lax.dot_general(left_side, right_side, (((1,), (1,)), ((), ())), preferre...]
    ppermute x40 -> x30, waiting for transfers between devices: 91.2 us -> 73.7 us  [swap_seq(): return lax.ppermute(values, 'seq', [(at, at ^ mask) for at in range(8)])]
    dot_general x5 -> x1, matrix products: 15.4 us -> 2.4 us  [product(): return jnp.dot(left_side, right_side, preferred_element_type=jnp.float32)]
    dot_general x5 -> x1, matrix products: 13.7 us -> 1.78 us  [rows_inner(): lax.dot_general(left_side, right_side, (((0,), (0,)), ((), ())), preferre...]
    rev x2 -> x0, local copies, waits for them, and re-layouts: 11.7 us -> none  [local_split(): split = jnp.where(core == 1, split[:, :, :, ::-1], split)]
    another operation x34 -> x10, other arithmetic: 13.4 us -> 4.93 us  [the longest x3 3.39 us: local_split(): ffn_local = jnp.stack([gate_weight, up_weight, down_weight]).astype(low)]
  transfers between devices with their start and end apart: 69 -> 56, of which waited for: 29 -> 25; matrix products, arithmetic and copies ran while one was open for 26% -> 10% of each run, Pallas kernels for 7% -> 29%
where the time goes in v2:
time: 350 us; the launch traced here: 344 us
  Pallas kernels  105 us (30%)
  waiting for transfers between devices  100 us (29%)
  starting transfers between devices  67.9 us (19%)
  other arithmetic  30.9 us (9%)
  local copies, waits for them, and re-layouts  19.4 us (6%)
  between operations  16.1 us (5%)
  matrix products  4.17 us (1%)
    ppermute x30, waiting for transfers between devices, swap_seq(): return lax.ppermute(values, 'seq', [(at, at ^ mask) for at in range(8)])  73.7 us
    ppermute x30, starting transfers between devices, swap_seq(): return lax.ppermute(values, 'seq', [(at, at ^ mask) for at in range(8)])  36.7 us
    ppermute x24, starting transfers between devices, swap_dp(): return lax.ppermute(values, 'dp', [(at, at ^ mask) for at in range(4)])  31.1 us
    pallas_call x3, Pallas kernels, gated(): pl.pallas_call(functools.partial(gated_kernel, count), grid=(2,), in_spec...  25.4 us
    pallas_call x1, Pallas kernels, attend_back(): pl.pallas_call(attend_back_kernel, grid=(2,), in_specs=[column(0), column...  23.7 us
    ppermute x24, waiting for transfers between devices, swap_dp(): return lax.ppermute(values, 'dp', [(at, at ^ mask) for at in range(4)])  20.4 us
    pallas_call x1, Pallas kernels, attend(): pl.pallas_call(attend_kernel, grid=(2,), in_specs=[column(0), column(2),...  13.9 us
    pallas_call x1, Pallas kernels, ffn_grads(): pl.pallas_call(ffn_grads_kernel, grid=(hidden // HIDDEN,), in_specs=[whol...  11.9 us
  transfers between devices with their start and end apart: 56, of which 25 were waited for; matrix products, arithmetic and copies ran while one was open for 10% of the time, Pallas kernels for 29%

profile of v2, /device:TPU:0, one launch (start us, length us, event | category | flops | bytes accessed | tf_op | source)
XLA Modules:
  0.0 344.1 jit_solution(12182597497314749566)
XLA Ops:
  14.9 3.7 %collective-permute-start.2 = (bf16[32,1664]{1,0:T(8,128)(2,1)S(1)}, bf16[32,1664]{1,0:T(8,128)(2,1)S(1)}, u32[]{:S(2)}, u32[]{:S(2)}) collective-permute-start(bf16[32,1664]{1,0:T(8,128)(2,1)S(1)} %get-tuple-element.165), channel_id=1, source_target_pairs={{0,4},{1,5},{2,6},{3,7},{4,0},{5,1},{6,2},{7,3},{8,12},{9,13},{10,... | collective-permute-start | bytes 319496 | tf_op jit(solution)/shard_map/ppermute | solution.py:414
  20.2 4.5 %collective-permute-done.2 = bf16[32,1664]{1,0:T(8,128)(2,1)S(1)} collective-permute-done((bf16[32,1664]{1,0:T(8,128)(2,1)S(1)}, bf16[32,1664]{1,0:T(8,128)(2,1)S(1)}, u32[]{:S(2)}, u32[]{:S(2)}) %collective-permute-start.2) | collective-permute-done | bytes 106528 | tf_op jit(solution)/shard_map/ppermute | solution.py:414
  24.8 3.2 collective-permute-done.3
  28.0 3.8 %collective-permute-start.5 = (bf16[176,1024]{1,0:T(8,128)(2,1)}, bf16[176,1024]{1,0:T(8,128)(2,1)S(1)}, u32[]{:S(2)}, u32[]{:S(2)}) collective-permute-start(bf16[176,1024]{1,0:T(8,128)(2,1)} %get-tuple-element.173), channel_id=1, source_target_pairs={{0,4},{1,5},{2,6},{3,7},{4,0},{5,1},{6,2},{7,3},{8,12},{9,13},{10,... | collective-permute-start | bytes 1081352 | tf_op jit(solution)/shard_map/ppermute | solution.py:414
  37.9 10.6 %collective-permute-done.5.refs_7_ = bf16[176,1024]{1,0:T(8,128)(2,1)S(1)} collective-permute-done((bf16[176,1024]{1,0:T(8,128)(2,1)}, bf16[176,1024]{1,0:T(8,128)(2,1)S(1)}, u32[]{:S(2)}, u32[]{:S(2)}) %collective-permute-start.5) | collective-permute-done | bytes 360480 | tf_op jit(solution)/shard_map/ppermute | solution.py:414
  48.5 3.1 fusion.3
  53.4 6.5 %collective-permute-done.6.refs_8_ = bf16[176,1024]{1,0:T(8,128)(2,1)S(1)} collective-permute-done((bf16[176,1024]{1,0:T(8,128)(2,1)S(1)}, bf16[176,1024]{1,0:T(8,128)(2,1)S(1)}, u32[]{:S(2)}, u32[]{:S(2)}) %collective-permute-start.6) | collective-permute-done | bytes 360480 | tf_op jit(solution)/shard_map/ppermute | solution.py:414
  75.0 6.1 %front.1 = (bf16[1024,768]{1,0:T(8,128)(2,1)}, bf16[1024,1024]{1,0:T(8,128)(2,1)}, f32[1024,768]{1,0:T(8,128)}) custom-call(s32[4]{0:T(128)} %pad_add_fusion.place, bf16[128,1536]{1,0:T(8,128)(2,1)} %copy-done.5, bf16[128,1536]{1,0:T(8,128)(2,1)} %copy-done.21, bf16[128,1536]{1,0:T(8,128)(2,1)} %copy-done.22, bf16[128,1536]{1,0:T(8,128)(2,1)} %copy-done.23, ...), custom_call_target="tpu_custom_call" | custom-call | flops 1610612736 | bytes 12582912 | tf_op jit(solution)/shard_map/front/pallas_call | solution.py:819
  81.1 13.9 %attend.1 = (bf16[512,256]{1,0:T(8,128)(2,1)}, bf16[512,256]{1,0:T(8,128)(2,1)}, bf16[1024,256]{1,0:T(8,128)(2,1)}, bf16[1024,256]{1,0:T(8,128)(2,1)}, bf16[1024...) custom-call(f32[1024,768]{1,0:T(8,128)} %get-tuple-element.185.q_in.k_in.v_in, ...), custom_call_target="tpu_custom_call" | custom-call | flops 4294967296 | bytes 7864320 | tf_op jit(solution)/shard_map/attend/pallas_call | solution.py:671
  104.4 4.4 %collective-permute-start.25 = (bf16[128,512]{1,0:T(8,128)(2,1)S(1)}, bf16[128,512]{1,0:T(8,128)(2,1)S(1)}, u32[]{:S(2)}, u32[]{:S(2)}) collective-permute-start(bf16[128,512]{1,0:T(8,128)(2,1)S(1)} %get-tuple-element.383), channel_id=1, source_target_pairs={{0,6},{1,7},{2,4},{3,5},{4,2},{5,3},{6,0},{7,1},{8,14},{9,15},{10,... | collective-permute-start | bytes 393224 | tf_op jit(solution)/shard_map/ppermute | solution.py:414
  108.8 3.1 place_rows.1
  111.9 3.8 %collective-permute-done.22.refs_1_.refs_7_ = bf16[256,1024]{1,0:T(8,128)(2,1)} collective-permute-done((bf16[256,1024]{1,0:T(8,128)(2,1)S(1)}, bf16[256,1024]{1,0:T(8,128)(2,1)}, u32[]{:S(2)}, u32[]{:S(2)}) %collective-permute-start.22) | collective-permute-done | bytes 524320 | tf_op jit(solution)/shard_map/ppermute | solution.py:418
  117.5 7.7 %collective-permute-done.24 = bf16[128,512]{1,0:T(8,128)(2,1)S(1)} collective-permute-done((bf16[128,512]{1,0:T(8,128)(2,1)}, bf16[128,512]{1,0:T(8,128)(2,1)S(1)}, u32[]{:S(2)}, u32[]{:S(2)}) %collective-permute-start.24) | collective-permute-done | bytes 131104 | tf_op jit(solution)/shard_map/ppermute | solution.py:414
  128.6 6.2 %all-gather.2.cloned.1.call-done.refs_2_.refs_4_ = bf16[3,1024,1024]{2,1,0:T(8,128)(2,1)} async-done(((bf16[3,128,1024]{2,1,0:T(8,128)(2,1)}), bf16[3,1024,1024]{2,1,0:T(8,128)(2,1)}) %all-gather.2.cloned.1.call-update) | async-done | bytes 6291472 | tf_op jit(solution)/shard_map/all_gather | solution.py:1250
  137.7 7.1 %gated.3 = (bf16[3,256,1024]{2,1,0:T(8,128)(2,1)}, f32[256,1024]{1,0:T(8,128)}) custom-call(bf16[256,1024]{1,0:T(8,128)(2,1)} %copy-done.10, bf16[256,1024]{1,0:T(8,128)(2,1)} %bitcast.171, bf16[3,1024,1024]{2,1,0:T(8,128)(2,1)} %all-gather.2.cloned.1.call-done.refs_2_.refs_4_), custom_call_target="tpu_custom_call" | custom-call | flops 2684354560 | bytes 9961472 | tf_op jit(solution)/shard_map/gated/pallas_call | solution.py:1044
  144.8 4.1 %collective-permute-done.26.refs_0_.refs_1_ = bf16[256,1024]{1,0:T(8,128)(2,1)S(1)} collective-permute-done((bf16[256,1024]{1,0:T(8,128)(2,1)S(1)}, bf16[256,1024]{1,0:T(8,128)(2,1)S(1)}, u32[]{:S(2)}, u32[]{:S(2)}) %collective-permute-start.26) | collective-permute-done | bytes 524320 | tf_op jit(solution)/shard_map/ppermute | solution.py:418
  151.6 11.4 %gated.4 = (bf16[3,256,1024]{2,1,0:T(8,128)(2,1)}, bf16[3,256,1024]{2,1,0:T(8,128)(2,1)}, bf16[256,1024]{1,0:T(8,128)(2,1)}, bf16[256,1024]{1,0:T(8,128)(2,1)}) custom-call(bf16[256,1024]{1,0:T(8,128)(2,1)} %copy-done.58, bf16[256,1024]{1,0:T(8,128)(2,1)} %copy-done.59, bf16[256,1024]{1,0:T(8,128)(2,1)} %copy-done.56, bf16[256,1024]{1,0:T(8,128)(2,1)} %copy-done.57, ...), custom_call_target="tpu_custom_call" | custom-call | flops 5368709120 | bytes 13631488 | tf_op jit(solution)/shard_map/gated/pallas_call | solution.py:1044
  165.0 7.0 %gated.5 = (bf16[3,256,1024]{2,1,0:T(8,128)(2,1)}, bf16[256,1024]{1,0:T(8,128)(2,1)}) custom-call(bf16[256,1024]{1,0:T(8,128)(2,1)} %copy-done.61, bf16[256,1024]{1,0:T(8,128)(2,1)} %collective-permute-done.22.refs_1_.refs_7_, bf16[3,1024,1024]{2,1,0:T(8,128)(2,1)} %all-gather.2.cloned.1.call-done.refs_2_.refs_4_), custom_call_target="tpu_custom_call" | custom-call | flops 2684354560 | bytes 9961472 | tf_op jit(solution)/shard_map/gated/pallas_call | solution.py:1044
  175.4 11.9 %ffn_grads.1 = bf16[3,1024,1024]{2,1,0:T(8,128)(2,1)} custom-call(bf16[256,1024]{1,0:T(8,128)(2,1)} %copy-done.10, bf16[256,1024]{1,0:T(8,128)(2,1)} %copy-done.58, bf16[256,1024]{1,0:T(8,128)(2,1)} %copy-done.59, bf16[256,1024]{1,0:T(8,128)(2,1)} %copy-done.61, bf16[256,1024]{1,0:T(8,128)(2,1)} %bitcast.172, bf16[256,1024]{1,0:T(8,128)(2,1)} %copy-done.56, ...), custom_call_target="tpu_custom_call" | custom-call | flops 6442450944 | bytes 20971520 | tf_op jit(solution)/shard_map/ffn_grads/pallas_call | solution.py:1089
  187.9 8.4 %collective-permute-done.29.near = bf16[256,1024]{1,0:T(8,128)(2,1)S(1)} collective-permute-done((bf16[256,1024]{1,0:T(8,128)(2,1)}, bf16[256,1024]{1,0:T(8,128)(2,1)S(1)}, u32[]{:S(2)}, u32[]{:S(2)}) %collective-permute-start.29) | collective-permute-done | bytes 524320 | tf_op jit(solution)/shard_map/ppermute | solution.py:418
  198.0 5.5 %middle_back.1 = (f32[256,1024]{1,0:T(8,128)}, bf16[256,1024]{1,0:T(8,128)(2,1)}, bf16[256,1024]{1,0:T(8,128)(2,1)}, f32[1,1024]{1,0:T(1,128)}) custom-call(f32[256,1024]{1,0:T(8,128)} %get-tuple-element.244.kept, bf16[256,1024]{1,0:T(8,128)(2,1)} %copy-done.17, bf16[256,1024]{1,0:T(8,128)(2,1)} %copy-done.18, bf16[256,1024]{1,0:T(8,128)(2,1)} %copy-done.16, ...), custom_call_target="tpu_custom_call" | custom-call | flops 536870912 | bytes 7864320 | tf_op jit(solution)/shard_map/middle_back/pallas_call | solution.py:984
  207.8 3.3 collective-permute-start.35
  211.1 5.2 %down.2 = (f32[256,1024]{1,0:T(8,128)}, bf16[256,1024]{1,0:T(8,128)(2,1)}, bf16[256,1024]{1,0:T(8,128)(2,1)}, bf16[256,1024]{1,0:T(8,128)(2,1)}) custom-call(bf16[3,256,1024]{2,1,0:T(8,128)(2,1)} %get-tuple-element.236.refs_8_.refs_0_, bf16[3,256,1024]{2,1,0:T(8,128)(2,1)} %get-tuple-element.237.refs_9_.refs_1_, ...), custom_call_target="tpu_custom_call" | custom-call | flops 2147483648 | bytes 6815744 | tf_op jit(solution)/shard_map/down/pallas_call | solution.py:1120
  218.9 3.0 collective-permute-done.34
  221.9 3.6 %collective-permute-done.35 = bf16[128,512]{1,0:T(8,128)(2,1)S(1)} collective-permute-done((bf16[128,512]{1,0:T(8,128)(2,1)S(1)}, bf16[128,512]{1,0:T(8,128)(2,1)S(1)}, u32[]{:S(2)}, u32[]{:S(2)}) %collective-permute-start.35) | collective-permute-done | bytes 131104 | tf_op jit(solution)/shard_map/ppermute | solution.py:414
  234.4 23.7 %attend_back.1 = (bf16[3,1024,256]{2,1,0:T(8,128)(2,1)}, f32[2,2,128]{2,1,0:T(2,128)}, f32[2,2,128]{2,1,0:T(2,128)}) custom-call(f32[1024,768]{1,0:T(8,128)} %get-tuple-element.185.q_in.k_in.v_in, f32[1024,768]{1,0:T(8,128)} %get-tuple-element.185.q_in.k_in.v_in, bf16[1024,256]{1,0:T(8,128)(2,1)} %get-tuple-element.188.qs_in, ...), custom_call_target="tpu_custom_call" | custom-call | flops 10737418240 | bytes 10485760 | tf_op jit(solution)/shard_map/attend_back/pallas_call | solution.py:725
  258.2 7.9 %tail.1 = (f32[512,1024]{1,0:T(8,128)}, bf16[512,1024]{1,0:T(8,128)(2,1)}, bf16[528,768]{1,0:T(8,128)(2,1)}, bf16[528,768]{1,0:T(8,128)(2,1)}) custom-call(s32[4]{0:T(128)} %pad_add_fusion.place, bf16[3,1024,256]{2,1,0:T(8,128)(2,1)} %get-tuple-element.271.dqkv, bf16[1024,768]{1,0:T(8,128)(2,1)} %get-tuple-element.272.weights, ...), custom_call_target="tpu_custom_call" | custom-call | flops 3221225472 | bytes 14680064 | tf_op jit(solution)/shard_map/tail/pallas_call | solution.py:928
  277.9 5.2 %collective-permute-start.44 = (bf16[128,1024]{1,0:T(8,128)(2,1)S(1)}, bf16[128,1024]{1,0:T(8,128)(2,1)S(1)}, u32[]{:S(2)}, u32[]{:S(2)}) collective-permute-start(bf16[128,1024]{1,0:T(8,128)(2,1)S(1)} %get-tuple-element.360), channel_id=1, source_target_pairs={{0,4},{1,5},{2,6},{3,7},{4,0},{5,1},{6,2},{7,3},{8,12},{9,13},{10,... | collective-permute-start | bytes 786440 | tf_op jit(solution)/shard_map/ppermute | solution.py:414
  283.0 3.1 collective-permute-start.45
  286.3 15.1 %collective-permute-done.44 = bf16[128,1024]{1,0:T(8,128)(2,1)S(1)} collective-permute-done((bf16[128,1024]{1,0:T(8,128)(2,1)S(1)}, bf16[128,1024]{1,0:T(8,128)(2,1)S(1)}, u32[]{:S(2)}, u32[]{:S(2)}) %collective-permute-start.44) | collective-permute-done | bytes 262176 | tf_op jit(solution)/shard_map/ppermute | solution.py:414
  304.8 4.6 %collective-permute-start.51 = (bf16[336,256]{1,0:T(8,128)(2,1)S(1)}, bf16[336,256]{1,0:T(8,128)(2,1)S(1)}, u32[]{:S(2)}, u32[]{:S(2)}) collective-permute-start(bf16[336,256]{1,0:T(8,128)(2,1)S(1)} %get-tuple-element.392), channel_id=1, source_target_pairs={{0,2},{1,3},{2,0},{3,1},{4,6},{5,7},{6,4},{7,5},{8,10},{9,11},{10,... | collective-permute-start | bytes 516104 | tf_op jit(solution)/shard_map/ppermute | solution.py:414
  317.0 7.4 %collective-permute-done.52 = bf16[336,256]{1,0:T(8,128)(2,1)S(1)} collective-permute-done((bf16[336,256]{1,0:T(8,128)(2,1)S(1)}, bf16[336,256]{1,0:T(8,128)(2,1)S(1)}, u32[]{:S(2)}, u32[]{:S(2)}) %collective-permute-start.52) | collective-permute-done | bytes 172064 | tf_op jit(solution)/shard_map/ppermute | solution.py:414
  (394 shorter events, 110.1 us)
Async XLA Ops:
  7.2 127.6 %all-gather.2.cloned.1.call-start = ((), (), s32[]{:S(2)}) async-start(), calls=%async_computation.1 | async-start | bytes 7077888 | tf_op jit(solution)/shard_map/all_gather | solution.py:1250
  28.0 20.5 %collective-permute-start.5 = (bf16[176,1024]{1,0:T(8,128)(2,1)}, bf16[176,1024]{1,0:T(8,128)(2,1)S(1)}, u32[]{:S(2)}, u32[]{:S(2)}) collective-permute-start(bf16[176,1024]{1,0:T(8,128)(2,1)} %get-tuple-element.173), channel_id=1, source_target_pairs={{0,4},{1,5},{2,6},{3,7},{4,0},{5,1},{6,2},{7,3},{8,12},{9,13},{10,... | collective-permute-start | bytes 1081352 | tf_op jit(solution)/shard_map/ppermute | solution.py:414
  31.9 21.5 %collective-permute-start.7 = (bf16[128,1536]{1,0:T(8,128)(2,1)S(1)}, bf16[128,1536]{1,0:T(8,128)(2,1)S(1)}, u32[]{:S(2)}, u32[]{:S(2)}) collective-permute-start(bf16[128,1536]{1,0:T(8,128)(2,1)S(1)} %pad_maximum_fusion.10.refs_0_), channel_id=1, source_target_pairs={{0,8},{8,0},{16,24},{24,16},{1,9},{9,1},{17,25},{25,17},{2,10},{10... | collective-permute-start | bytes 1179656 | tf_op jit(solution)/shard_map/ppermute | solution.py:418
  33.4 19.9 %collective-permute-start.8 = (bf16[128,1536]{1,0:T(8,128)(2,1)S(1)}, bf16[128,1536]{1,0:T(8,128)(2,1)S(1)}, u32[]{:S(2)}, u32[]{:S(2)}) collective-permute-start(bf16[128,1536]{1,0:T(8,128)(2,1)S(1)} %pad_maximum_fusion.10.refs_0_), channel_id=1, source_target_pairs={{0,16},{8,24},{16,0},{24,8},{1,17},{9,25},{17,1},{25,9},{2,18},{10... | collective-permute-start | bytes 1179656 | tf_op jit(solution)/shard_map/ppermute | solution.py:418
  34.9 18.4 %collective-permute-start.9 = (bf16[128,1536]{1,0:T(8,128)(2,1)S(1)}, bf16[128,1536]{1,0:T(8,128)(2,1)S(1)}, u32[]{:S(2)}, u32[]{:S(2)}) collective-permute-start(bf16[128,1536]{1,0:T(8,128)(2,1)S(1)} %pad_maximum_fusion.10.refs_0_), channel_id=1, source_target_pairs={{0,24},{8,16},{16,8},{24,0},{1,25},{9,17},{17,9},{25,1},{2,26},{10... | collective-permute-start | bytes 1179656 | tf_op jit(solution)/shard_map/ppermute | solution.py:418
  35.4 17.9 %collective-permute-start.4 = (bf16[176,1024]{1,0:T(8,128)(2,1)S(1)}, bf16[176,1024]{1,0:T(8,128)(2,1)S(1)}, u32[]{:S(2)}, u32[]{:S(2)}) collective-permute-start(bf16[176,1024]{1,0:T(8,128)(2,1)S(1)} %get-tuple-element.178.refs_5_), channel_id=1, source_target_pairs={{0,2},{1,3},{2,0},{3,1},{4,6},{5,7},{6,4},{7,5},{8,10},{9,11},{10,... | collective-permute-start | bytes 1081352 | tf_op jit(solution)/shard_map/ppermute | solution.py:414
  60.6 242.4 %reduce-scatter.2.cloned.1.call-start = ((), (), s32[]{:S(2)}) async-start(), calls=%async_computation.2 | async-start | bytes 7077888 | tf_op jit(solution)/shard_map/reduce_scatter | solution.py:1344
  68.5 27.8 %collective-permute-start.12 = (bf16[256,1024]{1,0:T(8,128)(2,1)S(1)}, bf16[256,1024]{1,0:T(8,128)(2,1)S(1)}, u32[]{:S(2)}, u32[]{:S(2)}) collective-permute-start(bf16[256,1024]{1,0:T(8,128)(2,1)S(1)} %bitcast.174), channel_id=1, source_target_pairs={{0,8},{8,0},{16,24},{24,16},{1,9},{9,1},{17,25},{25,17},{2,10},{10... | collective-permute-start | bytes 1572872 | tf_op jit(solution)/shard_map/ppermute | solution.py:418
  70.0 26.4 %collective-permute-start.13 = (bf16[256,1024]{1,0:T(8,128)(2,1)S(1)}, bf16[256,1024]{1,0:T(8,128)(2,1)S(1)}, u32[]{:S(2)}, u32[]{:S(2)}) collective-permute-start(bf16[256,1024]{1,0:T(8,128)(2,1)S(1)} %bitcast.175), channel_id=1, source_target_pairs={{0,16},{8,24},{16,0},{24,8},{1,17},{9,25},{17,1},{25,9},{2,18},{10... | collective-permute-start | bytes 1572872 | tf_op jit(solution)/shard_map/ppermute | solution.py:418
  71.5 23.5 %collective-permute-start.14 = (bf16[144,1024]{1,0:T(8,128)(2,1)S(1)}, bf16[144,1024]{1,0:T(8,128)(2,1)S(1)}, u32[]{:S(2)}, u32[]{:S(2)}) collective-permute-start(bf16[144,1024]{1,0:T(8,128)(2,1)S(1)} %constant_dynamic-update-slice_fusion.refs_0_), channel_id=1, source_target_pairs={{0,8},{8,0},{16,24},{24,16},{1,9},{9,1},{17,25},{25,17},{2,10},{10... | collective-permute-start | bytes 884744 | tf_op jit(solution)/shard_map/ppermute | solution.py:418
  72.0 24.3 %collective-permute-start.15 = (bf16[144,1024]{1,0:T(8,128)(2,1)S(1)}, bf16[144,1024]{1,0:T(8,128)(2,1)S(1)}, u32[]{:S(2)}, u32[]{:S(2)}) collective-permute-start(bf16[144,1024]{1,0:T(8,128)(2,1)S(1)} %constant_dynamic-update-slice_fusion.refs_0_), channel_id=1, source_target_pairs={{0,16},{8,24},{16,0},{24,8},{1,17},{9,25},{17,1},{25,9},{2,18},{10... | collective-permute-start | bytes 884744 | tf_op jit(solution)/shard_map/ppermute | solution.py:418
  72.5 23.8 %collective-permute-start.16 = (bf16[144,1024]{1,0:T(8,128)(2,1)S(1)}, bf16[144,1024]{1,0:T(8,128)(2,1)S(1)}, u32[]{:S(2)}, u32[]{:S(2)}) collective-permute-start(bf16[144,1024]{1,0:T(8,128)(2,1)S(1)} %constant_dynamic-update-slice_fusion.refs_0_), channel_id=1, source_target_pairs={{0,24},{8,16},{16,8},{24,0},{1,25},{9,17},{17,9},{25,1},{2,26},{10... | collective-permute-start | bytes 884744 | tf_op jit(solution)/shard_map/ppermute | solution.py:418
  100.7 15.0 %collective-permute-start.22 = (bf16[256,1024]{1,0:T(8,128)(2,1)S(1)}, bf16[256,1024]{1,0:T(8,128)(2,1)}, u32[]{:S(2)}, u32[]{:S(2)}) collective-permute-start(bf16[256,1024]{1,0:T(8,128)(2,1)S(1)} %bitcast.176), channel_id=1, source_target_pairs={{0,24},{8,16},{16,8},{24,0},{1,25},{9,17},{17,9},{25,1},{2,26},{10... | collective-permute-start | bytes 1572872 | tf_op jit(solution)/shard_map/ppermute | solution.py:418
  104.4 20.8 %collective-permute-start.24 = (bf16[128,512]{1,0:T(8,128)(2,1)}, bf16[128,512]{1,0:T(8,128)(2,1)S(1)}, u32[]{:S(2)}, u32[]{:S(2)}) collective-permute-start(bf16[128,512]{1,0:T(8,128)(2,1)} %get-tuple-element.386), channel_id=1, source_target_pairs={{0,4},{1,5},{2,6},{3,7},{4,0},{5,1},{6,2},{7,3},{8,12},{9,13},{10,... | collective-permute-start | bytes 393224 | tf_op jit(solution)/shard_map/ppermute | solution.py:414
  104.4 20.8 %collective-permute-start.25 = (bf16[128,512]{1,0:T(8,128)(2,1)S(1)}, bf16[128,512]{1,0:T(8,128)(2,1)S(1)}, u32[]{:S(2)}, u32[]{:S(2)}) collective-permute-start(bf16[128,512]{1,0:T(8,128)(2,1)S(1)} %get-tuple-element.383), channel_id=1, source_target_pairs={{0,6},{1,7},{2,4},{3,5},{4,2},{5,3},{6,0},{7,1},{8,14},{9,15},{10,... | collective-permute-start | bytes 393224 | tf_op jit(solution)/shard_map/ppermute | solution.py:414
  171.9 16.0 %collective-permute-start.31 = (bf16[256,1024]{1,0:T(8,128)(2,1)}, bf16[256,1024]{1,0:T(8,128)(2,1)S(1)}, u32[]{:S(2)}, u32[]{:S(2)}) collective-permute-start(bf16[256,1024]{1,0:T(8,128)(2,1)} %get-tuple-element.243), channel_id=1, source_target_pairs={{0,24},{8,16},{16,8},{24,0},{1,25},{9,17},{17,9},{25,1},{2,26},{10... | collective-permute-start | bytes 1572872 | tf_op jit(solution)/shard_map/ppermute | solution.py:418
  173.5 22.8 %collective-permute-start.29 = (bf16[256,1024]{1,0:T(8,128)(2,1)}, bf16[256,1024]{1,0:T(8,128)(2,1)S(1)}, u32[]{:S(2)}, u32[]{:S(2)}) collective-permute-start(bf16[256,1024]{1,0:T(8,128)(2,1)} %get-tuple-element.241), channel_id=1, source_target_pairs={{0,8},{8,0},{16,24},{24,16},{1,9},{9,1},{17,25},{25,17},{2,10},{10... | collective-permute-start | bytes 1572872 | tf_op jit(solution)/shard_map/ppermute | solution.py:418
  174.8 21.5 %collective-permute-start.30 = (bf16[256,1024]{1,0:T(8,128)(2,1)S(1)}, bf16[256,1024]{1,0:T(8,128)(2,1)S(1)}, u32[]{:S(2)}, u32[]{:S(2)}) collective-permute-start(bf16[256,1024]{1,0:T(8,128)(2,1)S(1)} %copy-done.60), channel_id=1, source_target_pairs={{0,16},{8,24},{16,0},{24,8},{1,17},{9,25},{17,1},{25,9},{2,18},{10... | collective-permute-start | bytes 1572872 | tf_op jit(solution)/shard_map/ppermute | solution.py:418
  206.5 19.0 %collective-permute-start.32 = (bf16[4,4,32,1024]{3,2,1,0:T(8,128)(2,1)}, bf16[4,4,32,1024]{3,2,1,0:T(8,128)(2,1)}, u32[]{:S(2)}, u32[]{:S(2)}) collective-permute-start(bf16[4,4,32,1024]{3,2,1,0:T(8,128)(2,1)} %get-tuple-element.350), channel_id=1, source_target_pairs={{0,1},{1,0},{2,3},{3,2},{4,5},{5,4},{6,7},{7,6},{8,9},{9,8},{10,11... | collective-permute-start | bytes 3145736 | tf_op jit(solution)/shard_map/ppermute | solution.py:414
  206.6 15.3 %collective-permute-start.34 = (bf16[128,512]{1,0:T(8,128)(2,1)S(1)}, bf16[128,512]{1,0:T(8,128)(2,1)S(1)}, u32[]{:S(2)}, u32[]{:S(2)}) collective-permute-start(bf16[128,512]{1,0:T(8,128)(2,1)S(1)} %get-tuple-element.377), channel_id=1, source_target_pairs={{0,4},{1,5},{2,6},{3,7},{4,0},{5,1},{6,2},{7,3},{8,12},{9,13},{10,... | collective-permute-start | bytes 393224 | tf_op jit(solution)/shard_map/ppermute | solution.py:414
  207.8 17.7 %collective-permute-start.35 = (bf16[128,512]{1,0:T(8,128)(2,1)S(1)}, bf16[128,512]{1,0:T(8,128)(2,1)S(1)}, u32[]{:S(2)}, u32[]{:S(2)}) collective-permute-start(bf16[128,512]{1,0:T(8,128)(2,1)S(1)} %get-tuple-element.375), channel_id=1, source_target_pairs={{0,6},{1,7},{2,4},{3,5},{4,2},{5,3},{6,0},{7,1},{8,14},{9,15},{10,... | collective-permute-start | bytes 393224 | tf_op jit(solution)/shard_map/ppermute | solution.py:414
  228.9 29.2 %collective-permute-start.37 = (bf16[4,32,1024]{2,1,0:T(8,128)(2,1)}, bf16[4,32,1024]{2,1,0:T(8,128)(2,1)S(1)}, u32[]{:S(2)}, u32[]{:S(2)}) collective-permute-start(bf16[4,32,1024]{2,1,0:T(8,128)(2,1)} %get-tuple-element.364), channel_id=1, source_target_pairs={{0,8},{8,0},{16,24},{24,16},{1,9},{9,1},{17,25},{25,17},{2,10},{10... | collective-permute-start | bytes 786440 | tf_op jit(solution)/shard_map/ppermute | solution.py:418
  229.8 28.4 %collective-permute-start.38 = (bf16[4,32,1024]{2,1,0:T(8,128)(2,1)S(1)}, bf16[4,32,1024]{2,1,0:T(8,128)(2,1)S(1)}, u32[]{:S(2)}, u32[]{:S(2)}) collective-permute-start(bf16[4,32,1024]{2,1,0:T(8,128)(2,1)S(1)} %get-tuple-element.363), channel_id=1, source_target_pairs={{0,16},{8,24},{16,0},{24,8},{1,17},{9,25},{17,1},{25,9},{2,18},{10... | collective-permute-start | bytes 786440 | tf_op jit(solution)/shard_map/ppermute | solution.py:418
  231.0 27.2 %collective-permute-start.39 = (bf16[4,32,1024]{2,1,0:T(8,128)(2,1)S(1)}, bf16[4,32,1024]{2,1,0:T(8,128)(2,1)S(1)}, u32[]{:S(2)}, u32[]{:S(2)}) collective-permute-start(bf16[4,32,1024]{2,1,0:T(8,128)(2,1)S(1)} %get-tuple-element.362), channel_id=1, source_target_pairs={{0,24},{8,16},{16,8},{24,0},{1,25},{9,17},{17,9},{25,1},{2,26},{10... | collective-permute-start | bytes 786440 | tf_op jit(solution)/shard_map/ppermute | solution.py:418
  232.4 25.8 %collective-permute-start.40 = (bf16[256,1024]{1,0:T(8,128)(2,1)}, bf16[256,1024]{1,0:T(8,128)(2,1)S(1)}, u32[]{:S(2)}, u32[]{:S(2)}) collective-permute-start(bf16[256,1024]{1,0:T(8,128)(2,1)} %get-tuple-element.269), channel_id=1, source_target_pairs={{0,8},{8,0},{16,24},{24,16},{1,9},{9,1},{17,25},{25,17},{2,10},{10... | collective-permute-start | bytes 1572872 | tf_op jit(solution)/shard_map/ppermute | solution.py:418
  233.3 24.9 %collective-permute-start.41 = (bf16[256,1024]{1,0:T(8,128)(2,1)}, bf16[256,1024]{1,0:T(8,128)(2,1)S(1)}, u32[]{:S(2)}, u32[]{:S(2)}) collective-permute-start(bf16[256,1024]{1,0:T(8,128)(2,1)} %get-tuple-element.270), channel_id=1, source_target_pairs={{0,16},{8,24},{16,0},{24,8},{1,17},{9,25},{17,1},{25,9},{2,18},{10... | collective-permute-start | bytes 1572872 | tf_op jit(solution)/shard_map/ppermute | solution.py:418
  273.0 28.5 %collective-permute-start.46 = (bf16[272,768]{1,0:T(8,128)(2,1)S(1)}, bf16[272,768]{1,0:T(8,128)(2,1)S(1)}, u32[]{:S(2)}, u32[]{:S(2)}) collective-permute-start(bf16[272,768]{1,0:T(8,128)(2,1)S(1)} %get-tuple-element.449), channel_id=1, source_target_pairs={{0,8},{8,0},{16,24},{24,16},{1,9},{9,1},{17,25},{25,17},{2,10},{10... | collective-permute-start | bytes 1253384 | tf_op jit(solution)/shard_map/ppermute | solution.py:418
  274.2 27.2 %collective-permute-start.47 = (bf16[272,768]{1,0:T(8,128)(2,1)S(1)}, bf16[272,768]{1,0:T(8,128)(2,1)S(1)}, u32[]{:S(2)}, u32[]{:S(2)}) collective-permute-start(bf16[272,768]{1,0:T(8,128)(2,1)S(1)} %get-tuple-element.450), channel_id=1, source_target_pairs={{0,16},{8,24},{16,0},{24,8},{1,17},{9,25},{17,1},{25,9},{2,18},{10... | collective-permute-start | bytes 1253384 | tf_op jit(solution)/shard_map/ppermute | solution.py:418
  275.1 27.9 %collective-permute-start.48 = (bf16[272,768]{1,0:T(8,128)(2,1)S(1)}, bf16[272,768]{1,0:T(8,128)(2,1)}, u32[]{:S(2)}, u32[]{:S(2)}) collective-permute-start(bf16[272,768]{1,0:T(8,128)(2,1)S(1)} %get-tuple-element.448), channel_id=1, source_target_pairs={{0,24},{8,16},{16,8},{24,0},{1,25},{9,17},{17,9},{25,1},{2,26},{10... | collective-permute-start | bytes 1253384 | tf_op jit(solution)/shard_map/ppermute | solution.py:418
  277.9 23.6 %collective-permute-start.44 = (bf16[128,1024]{1,0:T(8,128)(2,1)S(1)}, bf16[128,1024]{1,0:T(8,128)(2,1)S(1)}, u32[]{:S(2)}, u32[]{:S(2)}) collective-permute-start(bf16[128,1024]{1,0:T(8,128)(2,1)S(1)} %get-tuple-element.360), channel_id=1, source_target_pairs={{0,4},{1,5},{2,6},{3,7},{4,0},{5,1},{6,2},{7,3},{8,12},{9,13},{10,... | collective-permute-start | bytes 786440 | tf_op jit(solution)/shard_map/ppermute | solution.py:414
  283.0 18.5 %collective-permute-start.45 = (bf16[128,1024]{1,0:T(8,128)(2,1)S(1)}, bf16[128,1024]{1,0:T(8,128)(2,1)S(1)}, u32[]{:S(2)}, u32[]{:S(2)}) collective-permute-start(bf16[128,1024]{1,0:T(8,128)(2,1)S(1)} %get-tuple-element.359), channel_id=1, source_target_pairs={{0,6},{1,7},{2,4},{3,5},{4,2},{5,3},{6,0},{7,1},{8,14},{9,15},{10,... | collective-permute-start | bytes 786440 | tf_op jit(solution)/shard_map/ppermute | solution.py:414
  309.5 14.9 %collective-permute-start.52 = (bf16[336,256]{1,0:T(8,128)(2,1)S(1)}, bf16[336,256]{1,0:T(8,128)(2,1)S(1)}, u32[]{:S(2)}, u32[]{:S(2)}) collective-permute-start(bf16[336,256]{1,0:T(8,128)(2,1)S(1)} %get-tuple-element.393), channel_id=1, source_target_pairs={{0,4},{1,5},{2,6},{3,7},{4,0},{5,1},{6,2},{7,3},{8,12},{9,13},{10,... | collective-permute-start | bytes 516104 | tf_op jit(solution)/shard_map/ppermute | solution.py:414
  (91 other events, 748.6 us)
Sparse Core Ops, SparseCore 0:
  60.8 74.0 all-gather.1
  196.5 76.0 reduce-scatter.1
